TPU v7x, 256 devices: a whole 4x4x8 slice. The times are simulated.
256 devices in a mesh: slab: 128 (over z, y_lo, x, core), plane: 2 (over y_hi).
Axes of the slice: x: 4, y: 4 (y_hi: 2, y_lo: 2; y = y_hi * 2 + y_lo), z: 8, core: 2. Of those that a mesh axis runs over, the one named last changes fastest.
Arguments:
- probe_pos: bfloat16 [3, 32768], P(None, ('slab', 'plane')), may hold values from 0 to 2
- atom_pos: bfloat16 [3, 32768], P(None, ('slab', 'plane')), may hold values from 0 to 2
- atom_feat: bfloat16 [128, 32768], P(None, ('slab', 'plane')), may hold values from -6 to 6
- neighbours: int32 [32, 32768], P(None, ('slab', 'plane')), may hold values from 0 to 32767, as said below
- valid: int32 [32, 32768], P(None, ('slab', 'plane')), may hold values 0 or 1
- w_radial1: float32 [64, 8], replicated, may hold values from -2 to 2
- w_radial2: bfloat16 [640, 64], replicated, may hold values from -0.75 to 0.75
- readout: float32 [5, 128], replicated, may hold values from -0.5 to 0.5
- cotangent: float32 [32768], P(('slab', 'plane')), may hold values from -6 to 6
Outputs:
- density: float32 [32768], P(('slab', 'plane'))
- grad_feat: float32 [128, 32768], P(None, ('slab', 'plane'))
- grad_radial1: float32 [64, 8], replicated
- grad_radial2: float32 [640, 64], replicated
- grad_readout: float32 [5, 128], replicated
Inputs may be any that keep to these rules, and one draw needn't show every extreme that they name: `neighbours`: the atom of every slot of probe p lies in the slab of p (atoms a with a // 256 = p // 256) or in one of the two slabs beside it on the periodic cycle of slabs.
All inputs are finite; a program needn't handle non-finite values. No bound on the sum of `valid` on one device may be relied on, other than what follows from the above.
Results may differ from a plain program's by a relative error of at most 0.0049.
Values may be sent and summed in bfloat16 or wider, within the bound.
No kernel may reach another device: no remote copies, remote signals or barrier semaphores. Data moves between devices by JAX's collectives and lax.ppermute only.
A program may use at most 128 MiB of HBM per device.

v0:
```python
import math

import jax
import jax.numpy as jnp
from jax import lax
from jax.sharding import PartitionSpec as P

slab_width = 2.0
soften = 0.25


def padded(block, sides, width):
    for axis, dim in sides:
        count = lax.axis_size(axis)
        forward = [(i, i + 1) for i in range(count - 1)]
        forward.append((count - 1, 0))
        backward = [(target, source) for source, target in forward]
        low = lax.ppermute(
            lax.slice_in_dim(block, block.shape[dim] - width, None, axis=dim), axis, forward
        )
        high = lax.ppermute(lax.slice_in_dim(block, 0, width, axis=dim), axis, backward)
        block = jnp.concatenate([low, block, high], axis=dim)
    return block


def passed_along(block, axis, distance):
    devices = range(lax.axis_size(axis))
    route = [((i - distance) % len(devices), i) for i in devices]
    return lax.ppermute(block, axis, route)


def harmonics(along_x, along_y, along_z):
    sq_x = along_x * along_x
    sq_y = along_y * along_y
    sq_z = along_z * along_z
    root3 = math.sqrt(3.0)
    root15 = math.sqrt(15.0)
    root5 = math.sqrt(5.0)
    coef_a1 = math.sqrt(35.0 / 8.0)
    coef_a2 = math.sqrt(105.0)
    coef_a3 = math.sqrt(21.0 / 8.0)
    coef_a4 = math.sqrt(7.0) / 2.0
    coef_b1 = 3.0 * math.sqrt(35.0) / 2.0
    coef_b2 = 3.0 * math.sqrt(70.0) / 4.0
    coef_b3 = 3.0 * math.sqrt(5.0) / 2.0
    coef_b4 = 3.0 * math.sqrt(10.0) / 4.0
    rows_out = [
        jnp.ones_like(along_x),
        root3 * along_y,
        root3 * along_z,
        root3 * along_x,
        root15 * along_x * along_y,
        root15 * along_y * along_z,
        root5 / 2.0 * (3.0 * sq_z - 1.0),
        root15 * along_x * along_z,
        root15 / 2.0 * (sq_x - sq_y),
        coef_a1 * along_y * (3.0 * sq_x - sq_y),
        coef_a2 * along_x * along_y * along_z,
        coef_a3 * along_y * (5.0 * sq_z - 1.0),
        coef_a4 * along_z * (5.0 * sq_z - 3.0),
        coef_a3 * along_x * (5.0 * sq_z - 1.0),
        coef_a2 / 2.0 * along_z * (sq_x - sq_y),
        coef_a1 * along_x * (sq_x - 3.0 * sq_y),
        coef_b1 * along_x * along_y * (sq_x - sq_y),
        coef_b2 * along_y * along_z * (3.0 * sq_x - sq_y),
        coef_b3 * along_x * along_y * (7.0 * sq_z - 1.0),
        coef_b4 * along_y * along_z * (7.0 * sq_z - 3.0),
        0.375 * (35.0 * sq_z * sq_z - 30.0 * sq_z + 3.0),
        coef_b4 * along_x * along_z * (7.0 * sq_z - 3.0),
        coef_b3 / 2.0 * (sq_x - sq_y) * (7.0 * sq_z - 1.0),
        coef_b2 * along_x * along_z * (sq_x - 3.0 * sq_y),
        coef_b1 / 4.0 * (sq_x * (sq_x - 3.0 * sq_y) - sq_y * (3.0 * sq_x - sq_y)),
    ]
    return jnp.stack(rows_out)


def probe_block(
    features, atom_xyz, probe_xyz, offset, weight_mask, cot_block, w_radial1, w_radial2, readout
):
    slots, block_len = weight_mask.shape
    edge_count = slots * block_len
    channels = features.shape[0]
    degrees = readout.shape[0]
    probe_tile = jnp.broadcast_to(probe_xyz[:, None, :], (3, slots, block_len)).reshape(
        3, edge_count
    )
    delta_x = atom_xyz[0] - probe_tile[0]
    delta_y = atom_xyz[1] - probe_tile[1]
    delta_z = atom_xyz[2] + slab_width * offset.reshape(edge_count) - probe_tile[2]
    radius = jnp.sqrt(delta_x * delta_x + delta_y * delta_y + delta_z * delta_z + soften)
    sphere = harmonics(delta_x / radius, delta_y / radius, delta_z / radius)
    centres = 0.75 * jnp.arange(w_radial1.shape[1], dtype=jnp.float32)
    radial_basis = jnp.exp(-2.0 * (radius[None, :] - centres[:, None]) ** 2)
    preact = jnp.dot(w_radial1, radial_basis, precision=lax.Precision.HIGHEST)
    hidden = jax.nn.silu(preact).astype(jnp.bfloat16)
    radial = jnp.dot(w_radial2, hidden, preferred_element_type=jnp.float32).reshape(
        degrees, channels, edge_count
    )
    weight = weight_mask.reshape(edge_count) * (1.0 / math.sqrt(slots))
    feat_float = features.astype(jnp.float32)
    messages = (radial * feat_float[None] * weight[None, None, :]).reshape(
        degrees, channels, slots, block_len
    )
    sphere_rows = sphere.reshape(degrees * degrees, slots, block_len)
    density = jnp.zeros((block_len,), jnp.float32)
    grad_msg = []
    grad_read = []
    for degree in range(degrees):
        part_y = sphere_rows[degree * degree : (degree + 1) * (degree + 1)]
        moment = jnp.einsum(
            "kjp,cjp->kcp", part_y, messages[degree], precision=lax.Precision.HIGHEST
        )
        if degree == 0:
            density = jnp.sum(readout[0][:, None] * moment[0], axis=0)
            grad_mom = cot_block[None, None, :] * readout[0][None, :, None]
            grad_read.append(jnp.sum(cot_block[None, :] * moment[0], axis=1))
        else:
            squares = jnp.sum(moment * moment, axis=0)
            density = density + jnp.sum(readout[degree][:, None] * squares, axis=0)
            grad_mom = 2.0 * cot_block[None, None, :] * readout[degree][None, :, None] * moment
            grad_read.append(jnp.sum(cot_block[None, :] * squares, axis=1))
        grad_msg.append(
            jnp.einsum("kjp,kcp->cjp", part_y, grad_mom, precision=lax.Precision.HIGHEST)
        )
    grad_messages = jnp.stack(grad_msg).reshape(degrees, channels, edge_count)
    grad_features = jnp.sum(grad_messages * radial, axis=0) * weight[None, :]
    grad_radial = (
        (grad_messages * feat_float[None] * weight[None, None, :])
        .reshape(degrees * channels, edge_count)
        .astype(jnp.bfloat16)
    )
    grad_w2 = lax.dot_general(
        grad_radial, hidden, (((1,), (1,)), ((), ())), preferred_element_type=jnp.float32
    )
    grad_hidden = lax.dot_general(
        w_radial2, grad_radial, (((0,), (0,)), ((), ())), preferred_element_type=jnp.float32
    )
    logistic = jax.nn.sigmoid(preact)
    grad_pre = grad_hidden * logistic * (1.0 + preact * (1.0 - logistic))
    grad_w1 = lax.dot_general(
        grad_pre, radial_basis, (((1,), (1,)), ((), ())), precision=lax.Precision.HIGHEST
    )
    return (density, grad_features, grad_w1, grad_w2, jnp.stack(grad_read))


def shards(
    probe_pos, atom_pos, atom_feat, neighbours, valid, w_radial1, w_radial2, readout, cotangent
):
    channels = atom_feat.shape[0]
    atom_dev = atom_feat.shape[1]
    plane_count = lax.axis_size("plane")
    slab_count = lax.axis_size("slab")
    slab_index = lax.axis_index("slab")
    atom_slab = atom_dev * plane_count
    atom_pack = jnp.concatenate([atom_feat, atom_pos], axis=0)
    slab_pack = lax.all_gather(atom_pack, "plane", axis=1, tiled=True)
    window = padded(slab_pack, (("slab", 1),), atom_slab)
    window_feat = window[:channels]
    window_xyz = window[channels:]
    local_rows = (neighbours - (slab_index - 1) * atom_slab) % (slab_count * atom_slab)
    offsets = (local_rows // atom_slab - 1).astype(jnp.float32)
    slots, probe_dev = neighbours.shape
    block_len = 128
    count = probe_dev // block_len
    rows_blocks = local_rows.reshape(slots, count, block_len).transpose(1, 0, 2)
    offset_blocks = offsets.reshape(slots, count, block_len).transpose(1, 0, 2)
    mask_blocks = valid.astype(jnp.float32).reshape(slots, count, block_len).transpose(1, 0, 2)
    probe_blocks = probe_pos.astype(jnp.float32).reshape(3, count, block_len).transpose(1, 0, 2)
    cot_blocks = cotangent.reshape(count, block_len)

    def advance(totals, inputs):
        grad_window, total_w1, total_w2, total_read = totals
        atom_rows, offset, mask_float, probe_xyz, cot_block = inputs
        flat_rows = atom_rows.reshape(-1)
        features = jnp.take(window_feat, flat_rows, axis=1)
        atom_xyz = jnp.take(window_xyz, flat_rows, axis=1).astype(jnp.float32)
        density, grad_features, grad_w1, grad_w2, grad_read = probe_block(
            features,
            atom_xyz,
            probe_xyz,
            offset,
            mask_float,
            cot_block,
            w_radial1,
            w_radial2,
            readout,
        )
        grad_window = grad_window.at[:, flat_rows].add(grad_features)
        return (
            (grad_window, total_w1 + grad_w1, total_w2 + grad_w2, total_read + grad_read),
            density,
        )

    start_totals = (
        jnp.zeros((channels, 3 * atom_slab), jnp.float32),
        jnp.zeros(w_radial1.shape, jnp.float32),
        jnp.zeros(w_radial2.shape, jnp.float32),
        jnp.zeros(readout.shape, jnp.float32),
    )
    totals, densities = lax.scan(
        advance, start_totals, (rows_blocks, offset_blocks, mask_blocks, probe_blocks, cot_blocks)
    )
    grad_window = totals[0]
    lower_part = passed_along(grad_window[:, :atom_slab], "slab", -1)
    upper_part = passed_along(grad_window[:, 2 * atom_slab :], "slab", 1)
    owned_part = grad_window[:, atom_slab : 2 * atom_slab] + lower_part + upper_part
    grad_feat = lax.psum_scatter(owned_part, "plane", scatter_dimension=1, tiled=True)
    summed_w1, summed_w2, summed_read = lax.psum(
        (totals[1], totals[2], totals[3]), ("slab", "plane")
    )
    scale = 1.0 / math.sqrt(probe_dev * slab_count * plane_count)
    return (
        densities.reshape(-1),
        grad_feat,
        summed_w1 * scale,
        summed_w2 * scale,
        summed_read * scale,
    )


def solution(mesh):
    in_specs = (
        P(None, ("slab", "plane")),
        P(None, ("slab", "plane")),
        P(None, ("slab", "plane")),
        P(None, ("slab", "plane")),
        P(None, ("slab", "plane")),
        P(),
        P(),
        P(),
        P(("slab", "plane")),
    )
    out_specs = (P(("slab", "plane")), P(None, ("slab", "plane")), P(), P(), P())
    return jax.shard_map(shards, mesh=mesh, in_specs=in_specs, out_specs=out_specs, check_vma=False)
```

profile of v0, /device:TPU:1, one launch (start us, length us, event | category | flops | bytes accessed | tf_op | source)
XLA Modules:
  0.0 537.1 jit_solution(2991363688126804630)
XLA Ops:
  9.8 6.0 %all_gather.3 = bf16[131,256]{0,1:T(8,128)(2,1)S(1)} all-gather(bf16[131,128]{0,1:T(8,128)(2,1)S(1)} %pad_maximum_fusion), channel_id=1, replica_groups=mesh['slab'=128,'plane'=2] {'plane'}, dimensions={1}, use_global_device_ids=true | all-gather | bytes 100608 | tf_op jit(solution)/shard_map/all_gather | solution.py:156
  15.8 3.0 collective-permute-start
  24.4 12.1 %gather_fusion = bf16[4096,3]{1,0:T(8,128)(2,1)S(1)} fusion(bf16[3,768]{0,1:T(8,128)(2,1)S(1)} %slice.163, s32[4096]{0:T(1024)S(1)} %broadcast_clamp_fusion), kind=kCustom, calls=%fused_computation | custom fusion | bytes 65536 | tf_op jit(solution)/shard_map/while/body/eval_jaxpr/jit(_take)/gather | solution.py:176
  41.3 5.4 %fusion.59 = f32[4096,640]{0,1:T(8,128)} fusion(bf16[640,64]{0,1:T(8,128)(2,1)S(1)} %copy-done, f32[64,4096]{1,0:T(8,128)S(1)} %convolution_bitcast_fusion.1), kind=kOutput, calls=%fused_computation.167 | convolution fusion | flops 336855040 | bytes 11616256 | tf_op jit(solution)/shard_map/while/body/eval_jaxpr/dot_general | solution.py:96
  46.8 11.3 %copy.168 = f32[5,128,4096]{1,2,0:T(8,128)} copy(f32[5,128,4096]{2,1,0:T(8,128)} %bitcast.125) | data formatting | bytes 20971520 | tf_op jit(solution)/shard_map/while/body/eval_jaxpr/reshape | solution.py:96
  58.0 14.9 %gather_fusion.1 = bf16[4096,128]{1,0:T(8,128)(2,1)} fusion(bf16[128,768]{0,1:T(8,128)(2,1)S(1)} %slice.167, s32[4096]{0:T(1024)S(1)} %broadcast_clamp_fusion), kind=kCustom, calls=%fused_computation.1 | custom fusion | bytes 2113536 | tf_op jit(solution)/shard_map/while/body/eval_jaxpr/jit(_take)/gather | solution.py:175
  72.9 3.4 convert_bitcast_fusion
  76.3 6.1 %multiply_multiply_fusion = f32[5,128,4096]{1,2,0:T(8,128)S(1)} fusion(f32[5,128,4096]{1,2,0:T(8,128)} %copy.168, f32[4096]{0:T(1024)S(1)} %multiply_bitcast_fusion.1, f32[128,4096]{0,1:T(8,128)S(1)} %convert_bitcast_fusion), kind=kLoop, calls=%fused_computation.6 | loop fusion | flops 5242880 | bytes 23085056 | tf_op jit(solution)/shard_map/while/body/eval_jaxpr/mul | solution.py:101
  82.4 4.0 fusion.61
  86.4 5.2 fusion.5
  94.9 1.9 copy.172
  96.8 1.6 stack.108
  100.0 1.9 copy.174
  101.9 4.8 multiply_reduce_fusion.1
  106.8 3.1 multiply_reduce_fusion.4
  110.0 3.3 multiply_reduce_fusion.3
  113.3 3.1 multiply_reduce_fusion.2
  117.2 3.5 convolution_bitcast_fusion.5
  121.9 3.7 convolution_bitcast_fusion.4
  126.7 3.5 convolution_bitcast_fusion.3
  131.4 3.5 convolution_bitcast_fusion.2
  139.2 7.6 %broadcast_multiply_fusion = (f32[5,128,4096]{1,2,0:T(8,128)}, f32[128,4096]{0,1:T(8,128)}) fusion(f32[5,128,4096]{1,2,0:T(8,128)S(1)} %constant_dynamic-update-slice_fusion.3, f32[128,4096]{0,1:T(8,128)S(1)} %convert_bitcast_fusion, f32[5,128,4096]{1,2,0:T(8,128)S(1)} %bitcast.124), kind=kLoop, calls=%fused_computation.7 | loop fusion | flops 7340032 | bytes 35651584 | tf_op jit(solution)/shard_map/while/body/eval_jaxpr/mul | solution.py:128
  146.7 11.3 %copy.186 = f32[5,128,4096]{2,1,0:T(8,128)} copy(f32[5,128,4096]{1,2,0:T(8,128)} %get-tuple-element.109) | data formatting | bytes 20971520 | tf_op jit(solution)/shard_map/while/body/eval_jaxpr/mul | solution.py:128
  158.0 5.4 fusion
  163.4 2.1 fusion.2
  165.6 2.4 fusion.58
  167.9 24.6 %scatter_custom_fusion = f32[128,768]{0,1:T(8,128)S(1)} fusion(s32[4096]{0:T(1024)} %bitcast.154, f32[128,4096]{0,1:T(8,128)S(1)} %copy-done.4, f32[4096]{0:T(1024)S(1)} %multiply_bitcast_fusion.1, f32[]{:T(128)} %constant.170.clone.1), kind=kCustom, calls=%fused_computation.12 | custom fusion | flops 1048576 | bytes 2507264 | tf_op jit(solution)/shard_map/while/body/eval_jaxpr/scatter-add | solution.py:188
  193.8 4.9 collective-permute-start.2
  198.7 2.2 fusion.39
  200.9 80.1 %all-reduce = (f32[64,8]{0,1:T(8,128)S(1)}, f32[5,128]{1,0:T(8,128)S(1)}) all-reduce(f32[64,8]{0,1:T(8,128)S(1)} %fusion.39, f32[5,128]{1,0:T(8,128)S(1)} %stack.121), channel_id=1, replica_groups=mesh['slab'=128,'plane'=2] {'slab','plane'}, use_global_device_ids=true, to_apply=%region_12.13 | all-reduce | flops 1152 | bytes 9216 | tf_op jit(solution)/shard_map/psum | solution.py:208
  283.5 242.6 %all-reduce.3.cloned.1.call-done = f32[640,64]{0,1:T(8,128)} async-done(((f32[640,64]{0,1:T(8,128)}), f32[640,64]{0,1:T(8,128)}) %all-reduce.3.cloned.1.call-update) | async-done | bytes 163856 | tf_op jit(solution)/shard_map/psum | solution.py:208
  526.1 1.6 broadcast_multiply_fusion.1
  (119 shorter events, 30.6 us)
Async XLA Ops:
  8.0 33.3 %copy-start = (bf16[640,64]{0,1:T(8,128)(2,1)S(1)}, bf16[640,64]{0,1:T(8,128)(2,1)}, u32[]{:S(2)}) copy-start(bf16[640,64]{0,1:T(8,128)(2,1)} %param.15) | copy-start | bytes 245764
  8.0 518.1 %all-reduce.3.cloned.1.call-start = ((), (), s32[]{:S(2)}) async-start(), calls=%async_computation.2 | async-start | bytes 327680 | tf_op jit(solution)/shard_map/psum | solution.py:208
  15.8 8.4 %collective-permute-start = (bf16[131,256]{0,1:T(8,128)(2,1)S(1)}, bf16[131,256]{0,1:T(8,128)(2,1)S(1)}, u32[]{:S(2)}, u32[]{:S(2)}) collective-permute-start(bf16[131,256]{0,1:T(8,128)(2,1)S(1)} %all_gather.3), channel_id=1, source_target_pairs={{0,2},{2,4},{4,6},{6,8},{8,10},{10,12},{12,14},{14,16},{16,18},{18... | collective-permute-start | bytes 201224 | tf_op jit(solution)/shard_map/ppermute | solution.py:18
  18.8 5.5 %collective-permute-start.1 = (bf16[131,256]{0,1:T(8,128)(2,1)S(1)}, bf16[131,256]{0,1:T(8,128)(2,1)S(1)}, u32[]{:S(2)}, u32[]{:S(2)}) collective-permute-start(bf16[131,256]{0,1:T(8,128)(2,1)S(1)} %all_gather.3), channel_id=1, source_target_pairs={{2,0},{4,2},{6,4},{8,6},{10,8},{12,10},{14,12},{16,14},{18,16},{20... | collective-permute-start | bytes 201224 | tf_op jit(solution)/shard_map/ppermute | solution.py:21
  20.9 3.4 copy-start.12
  24.2 16.0 %copy-start.14 = (f32[8]{0:T(128)}, f32[8]{0:T(128)S(1)}, u32[]{:S(2)}) copy-start(f32[8]{0:T(128)S(1)} %iota_multiply_fusion) | copy-start | bytes 100
  36.5 3.8 copy-start.13
  38.5 8.3 %copy-start.10 = (f32[1,4096]{1,0:T(1,128)}, f32[1,4096]{1,0:T(1,128)S(1)}, u32[]{:S(2)}) copy-start(f32[1,4096]{1,0:T(1,128)S(1)} %get-tuple-element.150) | copy-start | bytes 49156
  41.3 5.4 %copy-start.5 = (f32[64,4096]{1,0:T(8,128)}, f32[64,4096]{1,0:T(8,128)S(1)}, u32[]{:S(2)}) copy-start(f32[64,4096]{1,0:T(8,128)S(1)} %convolution_bitcast_fusion.1) | copy-start | bytes 3145732
  101.9 4.9 copy-start.3
  106.8 3.2 copy-start.2
  106.8 3.2 copy-start.7
  109.9 3.4 copy-start.1
  109.9 3.4 copy-start.8
  113.2 3.2 copy-start.9
  113.2 3.2 copy-start.16
  113.3 3.2 copy-start.17
  113.3 3.2 copy-start.18
  113.3 3.2 copy-start.19
  113.3 3.2 copy-start.20
  113.3 3.2 copy-start.21
  113.3 3.2 copy-start.22
  135.0 2.2 slice-start
  136.2 2.5 slice-start.1
  136.8 2.4 slice-start.2
  158.0 5.4 %copy-start.6 = (f32[64,4096]{1,0:T(8,128)S(1)}, f32[64,4096]{1,0:T(8,128)}, u32[]{:S(2)}) copy-start(f32[64,4096]{1,0:T(8,128)} %copy-done.5) | copy-start | bytes 3145732
  165.5 2.4 copy-start.4
  167.9 30.7 %copy-start.11 = (f32[1,4096]{1,0:T(1,128)S(1)}, f32[1,4096]{1,0:T(1,128)}, u32[]{:S(2)}) copy-start(f32[1,4096]{1,0:T(1,128)} %copy-done.10) | copy-start | bytes 49156
  167.9 30.7 %copy-start.15 = (f32[8]{0:T(128)S(1)}, f32[8]{0:T(128)}, u32[]{:S(2)}) copy-start(f32[8]{0:T(128)} %copy-done.14) | copy-start | bytes 100
  192.5 89.7 %collective-permute-start.3 = (f32[128,256]{0,1:T(8,128)S(1)}, f32[128,256]{0,1:T(8,128)S(1)}, u32[]{:S(2)}, u32[]{:S(2)}) collective-permute-start(f32[128,256]{0,1:T(8,128)S(1)} %get-tuple-element.117), channel_id=1, source_target_pairs={{254,0},{0,2},{2,4},{4,6},{6,8},{8,10},{10,12},{12,14},{14,16},{16... | collective-permute-start | bytes 393224 | tf_op jit(solution)/shard_map/ppermute | solution.py:29
  193.8 88.5 %collective-permute-start.2 = (f32[128,256]{0,1:T(8,128)S(1)}, f32[128,256]{0,1:T(8,128)S(1)}, u32[]{:S(2)}, u32[]{:S(2)}) collective-permute-start(f32[128,256]{0,1:T(8,128)S(1)} %get-tuple-element.116), channel_id=1, source_target_pairs={{2,0},{4,2},{6,4},{8,6},{10,8},{12,10},{14,12},{16,14},{18,16},{20... | collective-permute-start | bytes 393224 | tf_op jit(solution)/shard_map/ppermute | solution.py:29
  281.6 246.1 %reduce-scatter.2.cloned.1.call-start = ((), (), s32[]{:S(2)}) async-start(), calls=%async_computation.1 | async-start | bytes 196608 | tf_op jit(solution)/shard_map/reduce_scatter | solution.py:207
Sparse Core Ops, SparseCore 0:
  281.7 244.2 all-reduce.2
Sparse Core Ops, SparseCore 1:
  284.6 12.7 reduce-scatter.1
where the time goes:
time: 545 us; the launch traced here: 537 us
  waiting for transfers between devices  243 us (45%)
  blocking collectives  86.1 us (16%)
  local copies, waits for them, and re-layouts  78.1 us (14%)
  other arithmetic  57.1 us (10%)
  matrix products  46.8 us (9%)
  between operations  16.6 us (3%)
  starting transfers between devices  9.81 us (2%)
    psum x1, waiting for transfers between devices, shards(): lax.psum((totals[1], totals[2], totals[3]), ('slab', 'plane'))  243 us
    psum x1, blocking collectives, shards(): lax.psum((totals[1], totals[2], totals[3]), ('slab', 'plane'))  80.1 us
    scatter-add x1, other arithmetic, advance(): grad_window = grad_window.at[:, flat_rows].add(grad_features)  24.6 us
    dot_general x5, matrix products, probe_block(): jnp.einsum('kjp,cjp->kcp', part_y, messages[degree], precision=lax.Precis...  19.5 us
    gather x1, local copies, waits for them, and re-layouts, advance(): features = jnp.take(window_feat, flat_rows, axis=1)  14.9 us
    dot_general x4, matrix products, probe_block(): jnp.einsum('kjp,kcp->cjp', part_y, grad_mom, precision=lax.Precision.HIGH...  14.1 us
    gather x2, local copies, waits for them, and re-layouts, advance(): atom_xyz = jnp.take(window_xyz, flat_rows, axis=1).astype(jnp.float32)  12.5 us
    mul x1, local copies, waits for them, and re-layouts, probe_block(): grad_messages * feat_float[None] * weight[None, None, :]  11.3 us
  transfers between devices with their start and end apart: 6, of which 1 were waited for; matrix products, arithmetic and copies ran while one was open for 2% of the time, Pallas kernels for 0%

commit v1 on v0

v1 whole, which is shorter than its diff:
```python
import functools
import math
import jax
import jax.numpy as jnp
import numpy as np
from jax import lax
from jax.experimental import pallas as pl
from jax.experimental.pallas import tpu as pltpu
from jax.sharding import Mesh
from jax.sharding import PartitionSpec as P

F32 = jnp.float32
BF16 = jnp.bfloat16
NT = (((1,), (1,)), ((), ()))
NN = (((1,), (0,)), ((), ()))
DEG_OF = [0] + [1] * 3 + [2] * 5 + [3] * 7 + [4] * 9
PACK_ROWS = 144
PAY_ROWS = 384


def dot(a, b, dims=NN):
    return lax.dot_general(a, b, dims, preferred_element_type=F32)


def harmonics(along_x, along_y, along_z):
    sq_x = along_x * along_x
    sq_y = along_y * along_y
    sq_z = along_z * along_z
    root3 = math.sqrt(3.0)
    root15 = math.sqrt(15.0)
    root5 = math.sqrt(5.0)
    coef_a1 = math.sqrt(35.0 / 8.0)
    coef_a2 = math.sqrt(105.0)
    coef_a3 = math.sqrt(21.0 / 8.0)
    coef_a4 = math.sqrt(7.0) / 2.0
    coef_b1 = 3.0 * math.sqrt(35.0) / 2.0
    coef_b2 = 3.0 * math.sqrt(70.0) / 4.0
    coef_b3 = 3.0 * math.sqrt(5.0) / 2.0
    coef_b4 = 3.0 * math.sqrt(10.0) / 4.0
    return [
        jnp.ones_like(along_x),
        root3 * along_y,
        root3 * along_z,
        root3 * along_x,
        root15 * along_x * along_y,
        root15 * along_y * along_z,
        root5 / 2.0 * (3.0 * sq_z - 1.0),
        root15 * along_x * along_z,
        root15 / 2.0 * (sq_x - sq_y),
        coef_a1 * along_y * (3.0 * sq_x - sq_y),
        coef_a2 * along_x * along_y * along_z,
        coef_a3 * along_y * (5.0 * sq_z - 1.0),
        coef_a4 * along_z * (5.0 * sq_z - 3.0),
        coef_a3 * along_x * (5.0 * sq_z - 1.0),
        coef_a2 / 2.0 * along_z * (sq_x - sq_y),
        coef_a1 * along_x * (sq_x - 3.0 * sq_y),
        coef_b1 * along_x * along_y * (sq_x - sq_y),
        coef_b2 * along_y * along_z * (3.0 * sq_x - sq_y),
        coef_b3 * along_x * along_y * (7.0 * sq_z - 1.0),
        coef_b4 * along_y * along_z * (7.0 * sq_z - 3.0),
        0.375 * (35.0 * sq_z * sq_z - 30.0 * sq_z + 3.0),
        coef_b4 * along_x * along_z * (7.0 * sq_z - 3.0),
        coef_b3 / 2.0 * (sq_x - sq_y) * (7.0 * sq_z - 1.0),
        coef_b2 * along_x * along_z * (sq_x - 3.0 * sq_y),
        coef_b1 / 4.0 * (sq_x * (sq_x - 3.0 * sq_y) - sq_y * (3.0 * sq_x - sq_y)),
    ]


def iota(shape, dim):
    return lax.broadcasted_iota(jnp.int32, shape, dim)


def kernel(
    low_ref, own_ref, high_ref, idx_ref, wgt_ref, probe_ref, cot_ref, w1_ref, w2_ref, w2t_ref, ro_ref,
    dens_ref, gwin_ref, pay_ref,
    oh_ref, feat_ref, pos_ref, sph_ref, rad_ref, sb_ref, dens_s, gro_s, gwin_s, gw2_s, gw1_s, radial_s, gr_s,
    *, unroll_a, unroll_c,
):
    groups = idx_ref.shape[0]

    def gather(g, carry):
        row = idx_ref[pl.ds(g, 1), :]
        total = None
        for part, src in enumerate((low_ref, own_ref, high_ref)):
            hot = jnp.where(iota((256, 256), 0) + 256 * part == row, 1.0, 0.0).astype(BF16)
            oh_ref[g, pl.ds(256 * part, 256), :] = hot
            piece = dot(src[...], hot)
            total = piece if total is None else total + piece
        feat_ref[g] = total[:128].astype(BF16)
        for i in range(3):
            pos_ref[i, pl.ds(g, 1), :] = total[128 + i : 129 + i]
        return carry

    lax.fori_loop(0, groups, gather, 0, unroll=unroll_a)

    dx = pos_ref[0] - probe_ref[0]
    dy = pos_ref[1] - probe_ref[1]
    idx = idx_ref[...]
    offset = (idx >= 256).astype(F32) + (idx >= 512).astype(F32) - 1.0
    dz = pos_ref[2] + 2.0 * offset - probe_ref[2]
    radius = jnp.sqrt(dx * dx + dy * dy + dz * dz + 0.25)
    rad_ref[...] = radius
    inv = 1.0 / radius
    for k, val in enumerate(harmonics(dx * inv, dy * inv, dz * inv)):
        top = val.astype(BF16).astype(F32)
        sph_ref[0, k] = top
        sph_ref[1, k] = val - top

    sb_ref[...] = jnp.zeros_like(sb_ref)
    gro_s[...] = jnp.zeros_like(gro_s)
    gwin_s[...] = jnp.zeros_like(gwin_s)
    gw2_s[...] = jnp.zeros_like(gw2_s)
    gw1_s[...] = jnp.zeros_like(gw1_s)

    w1 = w1_ref[...]
    w1_top = w1.astype(BF16).astype(F32)
    w1_cat = jnp.concatenate([w1_top, w1_top, w1 - w1_top, jnp.zeros_like(w1)], axis=1).astype(BF16)

    def block(g, carry):
        wgt = wgt_ref[pl.ds(g, 1), :]
        offs = rad_ref[pl.ds(g, 1), :] - 0.75 * iota((8, 256), 0).astype(F32)
        basis = jnp.exp(-2.0 * offs * offs)
        basis_top = basis.astype(BF16).astype(F32)
        basis_cat = jnp.concatenate(
            [basis_top, basis - basis_top, basis_top, jnp.zeros_like(basis)], axis=0
        ).astype(BF16)
        preact = dot(w1_cat, basis_cat)
        sig = 1.0 / (1.0 + jnp.exp(-preact))
        hidden = (preact * sig).astype(BF16)
        slope = sig * (1.0 + preact * (1.0 - sig))
        mask = iota((8, 256), 0) == iota((8, 256), 1) // 32
        zero8 = jnp.zeros((8, 256), F32)
        for half in range(2):
            def rows_of(k):
                return jnp.where(mask, sph_ref[half, k, pl.ds(g, 1), :], 0.0)

            for k in range(0, 24, 2):
                base = 128 * half + (8 * k if k < 16 else 8 * (k - 16))
                la, lb = DEG_OF[k], DEG_OF[k + 1]
                a, b = rows_of(k), rows_of(k + 1)
                if la == lb:
                    sb_ref[la, pl.ds(base, 16), :] = jnp.concatenate([a, b], axis=0).astype(BF16)
                else:
                    sb_ref[la, pl.ds(base, 16), :] = jnp.concatenate([a, zero8], axis=0).astype(BF16)
                    sb_ref[lb, pl.ds(base, 16), :] = jnp.concatenate([zero8, b], axis=0).astype(BF16)
            sb_ref[4, pl.ds(128 * half + 64, 16), :] = jnp.concatenate([rows_of(24), zero8], axis=0).astype(BF16)
        fw = feat_ref[g].astype(F32) * wgt
        mom_a = None
        for l in range(5):
            radial = dot(w2_ref[pl.ds(128 * l, 128), :], hidden)
            radial_s[l] = radial
            piece = dot((radial * fw).astype(BF16), sb_ref[l], NT)
            if l == 4:
                mom_b = piece
            else:
                mom_a = piece if mom_a is None else mom_a + piece
        mom_a = mom_a[:, :128] + mom_a[:, 128:]
        mom_b = mom_b[:, :128] + mom_b[:, 128:]
        cot = cot_ref[pl.ds(g, 1), :][:, :128]
        first = iota((128, 128), 1) < 8
        ro_a, ro_b = ro_ref[:, :128], ro_ref[:, 128:]
        sq_a = jnp.where(first, mom_a, mom_a * mom_a)
        sq_b = mom_b * mom_b
        dens_s[pl.ds(g, 1), :] = jnp.concatenate(
            [jnp.sum(sq_a * ro_a, axis=0, keepdims=True), jnp.sum(sq_b * ro_b, axis=0, keepdims=True)], axis=1
        )
        gro_s[:, :128] += sq_a * cot
        gro_s[:, 128:] += sq_b * cot
        gm_a = (jnp.where(first, 1.0, 2.0 * mom_a) * (ro_a * cot)).astype(BF16)
        gm_b = (2.0 * mom_b * (ro_b * cot)).astype(BF16)
        gm_a = jnp.concatenate([gm_a, gm_a], axis=1)
        gm_b = jnp.concatenate([gm_b, gm_b], axis=1)
        gf = None
        for l in range(5):
            gmsg = dot(gm_b if l == 4 else gm_a, sb_ref[l])
            piece = gmsg * radial_s[l]
            gf = piece if gf is None else gf + piece
            gr_s[pl.ds(128 * l, 128), :] = (gmsg * fw).astype(BF16)
        gf = (gf * wgt).astype(BF16)
        gwin_s[...] += dot(gf, oh_ref[g], NT)
        gr = gr_s[...]
        gw2_s[...] += dot(hidden, gr, NT)
        gpre = dot(w2t_ref[...], gr) * slope
        gw1_s[...] += dot(basis_cat, gpre.astype(BF16), NT)
        return carry

    lax.fori_loop(0, groups, block, 0, unroll=unroll_c)

    hi = lax.Precision.HIGHEST
    fold = jnp.where(iota((256, 128), 0) % 8 == iota((256, 128), 1), 1.0, 0.0)
    dens_ref[...] = lax.dot_general(dens_s[...], fold, NN, precision=hi, preferred_element_type=F32)
    for part in range(3):
        gwin_ref[part] = gwin_s[:, pl.ds(256 * part, 256)].astype(BF16)
    for l in range(5):
        pay_ref[pl.ds(64 * l, 64), :] = gw2_s[:, pl.ds(128 * l, 128)].astype(pay_ref.dtype)
    k_of = iota((8, 256), 1) // 8
    deg = (k_of >= 1).astype(jnp.int32) + (k_of >= 4) + (k_of >= 9) + (k_of >= 16)
    pick = jnp.where((iota((8, 256), 0) == deg) & (k_of < 25), 1.0, 0.0)
    gro = lax.dot_general(pick, gro_s[...], NT, precision=hi, preferred_element_type=F32)
    gw1 = gw1_s[:8, :] + gw1_s[8:16, :]
    gw1 = jnp.concatenate([gw1, jnp.zeros((8, 64), F32)], axis=1)
    pay_ref[pl.ds(320, 16), :] = jnp.concatenate([gro, gw1], axis=0).astype(pay_ref.dtype)
    pay_ref[pl.ds(336, 48), :] = jnp.zeros((48, 128), pay_ref.dtype)


def layer(low, own, high, idx, wgt, probe, cot, w1, w2, w2t, ro, unroll_a=2, unroll_c=1, pay_dtype=BF16):
    groups = idx.shape[0]
    return pl.pallas_call(
        functools.partial(kernel, unroll_a=unroll_a, unroll_c=unroll_c),
        out_shape=(
            jax.ShapeDtypeStruct((groups, 128), F32),
            jax.ShapeDtypeStruct((3, 128, 256), BF16),
            jax.ShapeDtypeStruct((PAY_ROWS, 128), pay_dtype),
        ),
        in_specs=[pl.BlockSpec(memory_space=pltpu.VMEM)] * 11,
        out_specs=[pl.BlockSpec(memory_space=pltpu.VMEM)] * 3,
        scratch_shapes=[
            pltpu.VMEM((groups, 768, 256), BF16),
            pltpu.VMEM((groups, 128, 256), BF16),
            pltpu.VMEM((3, groups, 256), F32),
            pltpu.VMEM((2, 25, groups, 256), F32),
            pltpu.VMEM((groups, 256), F32),
            pltpu.VMEM((5, 256, 256), BF16),
            pltpu.VMEM((groups, 256), F32),
            pltpu.VMEM((128, 256), F32),
            pltpu.VMEM((128, 768), F32),
            pltpu.VMEM((64, 640), F32),
            pltpu.VMEM((32, 64), F32),
            pltpu.VMEM((5, 128, 256), F32),
            pltpu.VMEM((640, 256), BF16),
        ],
        compiler_params=pltpu.CompilerParams(vmem_limit_bytes=40 << 20),
        name="probe_layer",
    )(low, own, high, idx, wgt, probe, cot, w1, w2, w2t, ro)


def prep(neighbours, valid, probe_pos, cotangent, readout, slab_index, slab_count, atom_slab):
    slots, probes = neighbours.shape
    groups = probes // 8
    idx = (neighbours - (slab_index - 1) * atom_slab) % (slab_count * atom_slab)
    idx = idx.T.reshape(groups, 8 * slots)
    wgt = (valid.astype(F32) * (1.0 / math.sqrt(slots))).T.reshape(groups, 8 * slots)
    probe = jnp.repeat(probe_pos.astype(F32).reshape(3, groups, 8), slots, axis=2)
    cot = jnp.tile(cotangent.reshape(groups, 1, 8), (1, 32, 1)).reshape(groups, 256)
    deg = jnp.array(DEG_OF + [5] * 7)
    pick = (deg[None, :] == jnp.arange(5)[:, None]).astype(F32)
    pick = jnp.repeat(pick, 8, axis=1)
    ro = jnp.einsum("lc,lk->ck", readout, pick, precision=lax.Precision.HIGHEST)
    return idx, wgt, probe, cot, ro


AXES = ("z", "ylo", "x", "core", "yhi")
SLAB = ("z", "ylo", "x", "core")
NEAR = ("ylo", "x", "core")
FAR = ("z", "yhi")


def spread_kernel(x_ref, o_ref):
    total = jnp.sum(x_ref[...].astype(F32), axis=0)
    o_ref[...] = jnp.broadcast_to(total[None], o_ref.shape).astype(o_ref.dtype)


def spread(x, copies):
    return pl.pallas_call(
        spread_kernel,
        out_shape=jax.ShapeDtypeStruct((copies,) + x.shape[1:], x.dtype),
        in_specs=[pl.BlockSpec(memory_space=pltpu.VMEM)],
        out_specs=pl.BlockSpec(memory_space=pltpu.VMEM),
        name="spread",
    )(x)


def finish_kernel(scale, x_ref, w1_ref, w2_ref, ro_ref):
    def part(start, rows):
        return x_ref[pl.ds(start, rows), :].astype(F32) * scale

    for l in range(5):
        w2_ref[pl.ds(128 * l, 128), :] = part(64 * l, 64).T
    ro_ref[...] = part(320, 8)[:5]
    w1_ref[...] = part(328, 8).T[:64]


def finish(x, scale):
    return pl.pallas_call(
        functools.partial(finish_kernel, scale),
        out_shape=(
            jax.ShapeDtypeStruct((64, 8), F32),
            jax.ShapeDtypeStruct((640, 64), F32),
            jax.ShapeDtypeStruct((5, 128), F32),
        ),
        in_specs=[pl.BlockSpec(memory_space=pltpu.VMEM)],
        out_specs=[pl.BlockSpec(memory_space=pltpu.VMEM)] * 3,
        name="finish",
    )(x)


def exchange(x, axes):
    return lax.all_to_all(x, axes, 0, 0, tiled=True)


def passed_along(block, distance):
    count = lax.axis_size(SLAB)
    return lax.ppermute(block, SLAB, [(i, (i + distance) % count) for i in range(count)])


def shards(probe_pos, atom_pos, atom_feat, neighbours, valid, w_radial1, w_radial2, readout, cotangent):
    slab_count = lax.axis_size(SLAB)
    slab_index = lax.axis_index(SLAB)
    planes = lax.axis_size("yhi")
    atom_dev = atom_feat.shape[1]
    atom_slab = atom_dev * planes
    pack = jnp.concatenate(
        [atom_feat, atom_pos, jnp.zeros((PACK_ROWS - 131, atom_dev), BF16)], axis=0
    )
    own = lax.all_gather(pack, "yhi", axis=1, tiled=True)
    low = passed_along(own, 1)
    high = passed_along(own, -1)
    idx, wgt, probe, cot, ro = prep(
        neighbours, valid, probe_pos, cotangent, readout, slab_index, slab_count, atom_slab
    )
    dens, gwin, pay = layer(
        low, own, high, idx, wgt, probe, cot, w_radial1, w_radial2, w_radial2.T, ro
    )
    density = dens[:, :8].reshape(-1)
    from_high = passed_along(gwin[0], -1)
    from_low = passed_along(gwin[2], 1)
    near, far = lax.axis_size(NEAR), lax.axis_size(FAR)
    part = exchange(pay.reshape(near, PAY_ROWS // near, 128), NEAR)
    part = exchange(spread(part, far), FAR)
    slab_sum = gwin[1].astype(F32) + from_high.astype(F32) + from_low.astype(F32)
    plane = lax.axis_index("yhi")
    mine = lax.dynamic_slice_in_dim(slab_sum, plane * atom_dev, atom_dev, 1)
    other = lax.dynamic_slice_in_dim(slab_sum, (1 - plane) * atom_dev, atom_dev, 1)
    got = lax.ppermute(other.astype(BF16), "yhi", [(0, 1), (1, 0)])
    grad_feat = mine + got.astype(F32)
    part = exchange(spread(part, near), NEAR)
    scale = 1.0 / math.sqrt(neighbours.shape[1] * slab_count * planes)
    grad_w1, grad_w2, grad_ro = finish(part.reshape(PAY_ROWS, 128), scale)
    return density, grad_feat, grad_w1, grad_w2, grad_ro


def solution(mesh):
    fine = Mesh(np.asarray(mesh.devices).reshape(8, 2, 4, 2, 2), AXES)
    flat = P(None, AXES)
    in_specs = (flat, flat, flat, flat, flat, P(), P(), P(), P(AXES))
    out_specs = (P(AXES), flat, P(), P(), P())
    return jax.shard_map(shards, mesh=fine, in_specs=in_specs, out_specs=out_specs, check_vma=False)
```

time: 545 us -> 99.4 us (0.18); the launches traced: 537 us -> 98.7 us
  waiting for transfers between devices: 243 us -> 15.4 us
  blocking collectives: 86.1 us -> 5.77 us
  local copies, waits for them, and re-layouts: 78.1 us -> 11.3 us
  other arithmetic: 57.1 us -> 1.53 us
  matrix products: 46.8 us -> 0.32 us
  Pallas kernels: 0 us -> 31.4 us
  starting transfers between devices: 9.81 us -> 32.1 us
  between operations: 16.6 us -> 0.84 us
    psum x1 -> x0, waiting for transfers between devices: 243 us -> none  [shards(): lax.psum((totals[1], totals[2], totals[3]), ('slab', 'plane'))]
    psum x1 -> x0, blocking collectives: 80.1 us -> none  [shards(): lax.psum((totals[1], totals[2], totals[3]), ('slab', 'plane'))]
    dot_general x14 -> x1, matrix products: 46.8 us -> 0.32 us  [prep(): ro = jnp.einsum('lc,lk->ck', readout, pick, precision=lax.Precision.HIGHEST)]
    pallas_call x0 -> x4, Pallas kernels: none -> 31.4 us  [the longest x1 26.5 us: layer(): pl.pallas_call(functools.partial(kernel, unroll_a=unroll_a, unroll_c=unro...]
    gather x3 -> x0, local copies, waits for them, and re-layouts: 27.4 us -> none  [the longest x1 14.9 us: advance(): features = jnp.take(window_feat, flat_rows, axis=1)]
    scatter-add x1 -> x0, other arithmetic: 24.6 us -> none  [advance(): grad_window = grad_window.at[:, flat_rows].add(grad_features)]
    all_to_all x0 -> x3, starting transfers between devices: none -> 23.7 us  [exchange(): return lax.all_to_all(x, axes, 0, 0, tiled=True)]
    mul x12 -> x0, other arithmetic: 20.8 us -> none  [the longest x1 7.55 us: probe_block(): grad_messages * feat_float[None] * weight[None, None, :]]
  transfers between devices with their start and end apart: 6 -> 8, of which waited for: 1 -> 3; matrix products, arithmetic and copies ran while one was open for 2% -> 3% of each run, Pallas kernels for 0% -> 3%
where the time goes in v1:
time: 99.4 us; the launch traced here: 98.7 us
  starting transfers between devices  32.1 us (32%)
  Pallas kernels  31.4 us (32%)
  waiting for transfers between devices  15.4 us (15%)
  local copies, waits for them, and re-layouts  11.3 us (11%)
  blocking collectives  5.77 us (6%)
  other arithmetic  1.53 us (2%)
    pallas_call x1, Pallas kernels, layer(): pl.pallas_call(functools.partial(kernel, unroll_a=unroll_a, unroll_c=unro...  26.5 us
    all_to_all x3, starting transfers between devices, exchange(): return lax.all_to_all(x, axes, 0, 0, tiled=True)  23.7 us
    all_to_all x3, waiting for transfers between devices, exchange(): return lax.all_to_all(x, axes, 0, 0, tiled=True)  15.4 us
    unnamed x30, local copies, waits for them, and re-layouts  9.49 us
    all_gather x1, blocking collectives, shards(): own = lax.all_gather(pack, 'yhi', axis=1, tiled=True)  5.77 us
    ppermute x4, starting transfers between devices, passed_along(): lax.ppermute(block, SLAB, [(i, (i + distance) % count) for i in range(cou...  5.42 us
    pallas_call x2, Pallas kernels, spread(): pl.pallas_call(spread_kernel, out_shape=jax.ShapeDtypeStruct((copies,) +...  3.09 us
    ppermute x1, starting transfers between devices, shards(): got = lax.ppermute(other.astype(BF16), 'yhi', [(0, 1), (1, 0)])  2.95 us
  transfers between devices with their start and end apart: 8, of which 3 were waited for; matrix products, arithmetic and copies ran while one was open for 3% of the time, Pallas kernels for 3%

profile of v1, /device:TPU:1, one launch (start us, length us, event | category | flops | bytes accessed | tf_op | source)
XLA Modules:
  0.0 98.7 jit_solution(13492167871031810860)
XLA Ops:
  0.7 0.6 copy-done.9
  1.3 0.8 maximum_maximum_fusion
  2.2 5.8 %all_gather.3.own_ref = bf16[144,256]{1,0:T(8,128)(2,1)S(1)} all-gather(bf16[144,128]{1,0:T(8,128)(2,1)S(1)} %maximum_maximum_fusion), channel_id=1, replica_groups=mesh['z'=8,'ylo'=2,'x'=4,'core'=2,'yhi'=2] {'yhi'}, dimensions={1}, use_global_device_ids=true | all-gather | bytes 110592 | tf_op jit(solution)/shard_map/all_gather | solution.py:315
  8.0 3.0 %collective-permute-start = (bf16[144,256]{1,0:T(8,128)(2,1)S(1)}, bf16[144,256]{1,0:T(8,128)(2,1)S(1)}, u32[]{:S(2)}, u32[]{:S(2)}) collective-permute-start(bf16[144,256]{1,0:T(8,128)(2,1)S(1)} %all_gather.3.own_ref), channel_id=1, source_target_pairs={{0,2},{2,4},{4,6},{6,8},{8,10},{10,12},{12,14},{14,16},{16,18},{18... | collective-permute-start | bytes 221192 | tf_op jit(solution)/shard_map/ppermute | solution.py:303
  10.9 0.6 collective-permute-start.1
  11.6 0.7 copy-done.12
  12.4 0.5 copy-done.11
  13.1 0.7 copy-done.6
  13.9 0.3 convolution_bitcast_fusion.ro_ref
  14.2 0.4 copy-done.7
  14.8 0.6 copy-done.10
  15.7 0.8 copy-done.1
  16.9 0.6 copy-done.8
  17.6 26.5 %probe_layer.1 = (f32[16,128]{1,0:T(8,128)S(1)}, bf16[3,128,256]{2,1,0:T(8,128)(2,1)S(1)}, bf16[384,128]{1,0:T(8,128)(2,1)}) custom-call(bf16[144,256]{1,0:T(8,128)(2,1)S(1)} %collective-permute-done.low_ref, bf16[144,256]{1,0:T(8,128)(2,1)S(1)} %all_gather.3.own_ref, bf16[144,256]{1,0:T(8,128)(2,1)S(1)} %collective-permute-done.1.high_ref, ...), custom_call_target="tpu_custom_call" | custom-call | tf_op jit(solution)/shard_map/probe_layer/pallas_call | solution.py:208
  44.1 9.3 %all-to-all-start = ((bf16[16,24,128]{2,1,0:T(8,128)(2,1)}), bf16[16,24,128]{2,1,0:T(8,128)(2,1)S(1)}, u32[]{:S(2)}, u32[]{:S(2)}) async-start(bf16[16,24,128]{2,1,0:T(8,128)(2,1)} %bitcast.8), calls=%async_computation | async-start | bytes 196608 | tf_op jit(solution)/shard_map/all_to_all | solution.py:298
  53.7 1.5 %collective-permute-start.3 = (bf16[128,256]{1,0:T(8,128)(2,1)S(1)}, bf16[128,256]{1,0:T(8,128)(2,1)S(1)}, u32[]{:S(2)}, u32[]{:S(2)}) collective-permute-start(bf16[128,256]{1,0:T(8,128)(2,1)S(1)} %get-tuple-element.28), channel_id=1, source_target_pairs={{0,2},{2,4},{4,6},{6,8},{8,10},{10,12},{12,14},{14,16},{16,18},{18... | collective-permute-start | bytes 196616 | tf_op jit(solution)/shard_map/ppermute | solution.py:303
  55.2 4.1 %all-to-all-done.x_ref = bf16[16,24,128]{2,1,0:T(8,128)(2,1)S(1)} async-done(((bf16[16,24,128]{2,1,0:T(8,128)(2,1)}), bf16[16,24,128]{2,1,0:T(8,128)(2,1)S(1)}, u32[]{:S(2)}, u32[]{:S(2)}) %all-to-all-start) | async-done | bytes 98336 | tf_op jit(solution)/shard_map/all_to_all | solution.py:298
  59.3 0.6 copy-done.3
  59.9 1.5 %spread.2 = bf16[16,24,128]{2,1,0:T(8,128)(2,1)} custom-call(bf16[16,24,128]{2,1,0:T(8,128)(2,1)} %copy-done.3), custom_call_target="tpu_custom_call" | custom-call | tf_op jit(solution)/shard_map/spread/pallas_call | solution.py:264
  61.5 9.2 %all-to-all-start.1 = ((bf16[16,24,128]{2,1,0:T(8,128)(2,1)}), bf16[16,24,128]{2,1,0:T(8,128)(2,1)S(1)}, u32[]{:S(2)}, u32[]{:S(2)}) async-start(bf16[16,24,128]{2,1,0:T(8,128)(2,1)} %spread.2), calls=%async_computation.1 | async-start | bytes 196608 | tf_op jit(solution)/shard_map/all_to_all | solution.py:298
  70.8 3.0 %collective-permute-start.4 = (bf16[128,128]{1,0:T(8,128)(2,1)S(1)}, bf16[128,128]{1,0:T(8,128)(2,1)S(1)}, u32[]{:S(2)}, u32[]{:S(2)}) collective-permute-start(bf16[128,128]{1,0:T(8,128)(2,1)S(1)} %dynamic-slice_convert_fusion), channel_id=1, source_target_pairs={{0,1},{1,0},{2,3},{3,2},{4,5},{5,4},{6,7},{7,6},{8,9},{9,8},{10,11... | collective-permute-start | bytes 98312 | tf_op jit(solution)/shard_map/ppermute | solution.py:334
  73.7 0.6 reshape.50
  74.3 6.1 %all-to-all-done.1.x_ref = bf16[16,24,128]{2,1,0:T(8,128)(2,1)S(1)} async-done(((bf16[16,24,128]{2,1,0:T(8,128)(2,1)}), bf16[16,24,128]{2,1,0:T(8,128)(2,1)S(1)}, u32[]{:S(2)}, u32[]{:S(2)}) %all-to-all-start.1) | async-done | bytes 98336 | tf_op jit(solution)/shard_map/all_to_all | solution.py:298
  80.4 0.6 copy-done.2
  81.0 1.5 %spread.3 = bf16[16,24,128]{2,1,0:T(8,128)(2,1)} custom-call(bf16[16,24,128]{2,1,0:T(8,128)(2,1)} %copy-done.2), custom_call_target="tpu_custom_call" | custom-call | tf_op jit(solution)/shard_map/spread/pallas_call | solution.py:264
  82.6 5.3 %all-to-all-start.2 = ((bf16[16,24,128]{2,1,0:T(8,128)(2,1)}), bf16[16,24,128]{2,1,0:T(8,128)(2,1)S(1)}, u32[]{:S(2)}, u32[]{:S(2)}) async-start(bf16[16,24,128]{2,1,0:T(8,128)(2,1)} %spread.3), calls=%async_computation.2 | async-start | bytes 196608 | tf_op jit(solution)/shard_map/all_to_all | solution.py:298
  87.9 0.6 convert_add_fusion.1
  88.5 5.3 %all-to-all-done.2 = bf16[16,24,128]{2,1,0:T(8,128)(2,1)S(1)} async-done(((bf16[16,24,128]{2,1,0:T(8,128)(2,1)}), bf16[16,24,128]{2,1,0:T(8,128)(2,1)S(1)}, u32[]{:S(2)}, u32[]{:S(2)}) %all-to-all-start.2) | async-done | bytes 98336 | tf_op jit(solution)/shard_map/all_to_all | solution.py:298
  93.8 0.6 copy-done.4
  94.4 1.8 %finish.1 = (f32[64,8]{1,0:T(8,128)}, f32[640,64]{1,0:T(8,128)}, f32[5,128]{1,0:T(8,128)}) custom-call(bf16[384,128]{1,0:T(8,128)(2,1)} %bitcast.25), custom_call_target="tpu_custom_call" | custom-call | tf_op jit(solution)/shard_map/finish/pallas_call | solution.py:284
  96.2 1.8 %copy.30 = f32[640,64]{0,1:T(8,128)} copy(f32[640,64]{1,0:T(8,128)} %get-tuple-element.25) | data formatting | bytes 327680
  98.0 0.7 copy.29
  (44 shorter events, 1.8 us)
Async XLA Ops:
  0.6 13.2 %copy-start = (f32[5,128]{1,0:T(8,128)S(1)}, f32[5,128]{1,0:T(8,128)}, u32[]{:S(2)}) copy-start(f32[5,128]{1,0:T(8,128)} %param.17) | copy-start | bytes 7684
  0.7 0.7 copy-start.9
  8.0 9.6 %collective-permute-start = (bf16[144,256]{1,0:T(8,128)(2,1)S(1)}, bf16[144,256]{1,0:T(8,128)(2,1)S(1)}, u32[]{:S(2)}, u32[]{:S(2)}) collective-permute-start(bf16[144,256]{1,0:T(8,128)(2,1)S(1)} %all_gather.3.own_ref), channel_id=1, source_target_pairs={{0,2},{2,4},{4,6},{6,8},{8,10},{10,12},{12,14},{14,16},{16,18},{18... | collective-permute-start | bytes 221192 | tf_op jit(solution)/shard_map/ppermute | solution.py:303
  10.9 6.7 %collective-permute-start.1 = (bf16[144,256]{1,0:T(8,128)(2,1)S(1)}, bf16[144,256]{1,0:T(8,128)(2,1)S(1)}, u32[]{:S(2)}, u32[]{:S(2)}) collective-permute-start(bf16[144,256]{1,0:T(8,128)(2,1)S(1)} %all_gather.3.own_ref), channel_id=1, source_target_pairs={{0,254},{2,0},{4,2},{6,4},{8,6},{10,8},{12,10},{14,12},{16,14},{18... | collective-permute-start | bytes 221192 | tf_op jit(solution)/shard_map/ppermute | solution.py:303
  11.6 0.7 copy-start.12
  12.3 0.7 copy-start.11
  13.1 0.7 copy-start.6
  13.8 0.7 copy-start.7
  14.7 0.7 copy-start.10
  15.6 0.9 copy-start.1
  16.8 0.7 copy-start.8
  44.1 15.2 %all-to-all-start = ((bf16[16,24,128]{2,1,0:T(8,128)(2,1)}), bf16[16,24,128]{2,1,0:T(8,128)(2,1)S(1)}, u32[]{:S(2)}, u32[]{:S(2)}) async-start(bf16[16,24,128]{2,1,0:T(8,128)(2,1)} %bitcast.8), calls=%async_computation | async-start | bytes 196608 | tf_op jit(solution)/shard_map/all_to_all | solution.py:298
  53.4 17.3 %collective-permute-start.2 = (bf16[128,256]{1,0:T(8,128)(2,1)S(1)}, bf16[128,256]{1,0:T(8,128)(2,1)S(1)}, u32[]{:S(2)}, u32[]{:S(2)}) collective-permute-start(bf16[128,256]{1,0:T(8,128)(2,1)S(1)} %get-tuple-element.27), channel_id=1, source_target_pairs={{0,254},{2,0},{4,2},{6,4},{8,6},{10,8},{12,10},{14,12},{16,14},{18... | collective-permute-start | bytes 196616 | tf_op jit(solution)/shard_map/ppermute | solution.py:303
  53.7 17.0 %collective-permute-start.3 = (bf16[128,256]{1,0:T(8,128)(2,1)S(1)}, bf16[128,256]{1,0:T(8,128)(2,1)S(1)}, u32[]{:S(2)}, u32[]{:S(2)}) collective-permute-start(bf16[128,256]{1,0:T(8,128)(2,1)S(1)} %get-tuple-element.28), channel_id=1, source_target_pairs={{0,2},{2,4},{4,6},{6,8},{8,10},{10,12},{12,14},{14,16},{16,18},{18... | collective-permute-start | bytes 196616 | tf_op jit(solution)/shard_map/ppermute | solution.py:303
  59.3 0.6 copy-start.3
  61.5 18.9 %all-to-all-start.1 = ((bf16[16,24,128]{2,1,0:T(8,128)(2,1)}), bf16[16,24,128]{2,1,0:T(8,128)(2,1)S(1)}, u32[]{:S(2)}, u32[]{:S(2)}) async-start(bf16[16,24,128]{2,1,0:T(8,128)(2,1)} %spread.2), calls=%async_computation.1 | async-start | bytes 196608 | tf_op jit(solution)/shard_map/all_to_all | solution.py:298
  70.8 17.1 %collective-permute-start.4 = (bf16[128,128]{1,0:T(8,128)(2,1)S(1)}, bf16[128,128]{1,0:T(8,128)(2,1)S(1)}, u32[]{:S(2)}, u32[]{:S(2)}) collective-permute-start(bf16[128,128]{1,0:T(8,128)(2,1)S(1)} %dynamic-slice_convert_fusion), channel_id=1, source_target_pairs={{0,1},{1,0},{2,3},{3,2},{4,5},{5,4},{6,7},{7,6},{8,9},{9,8},{10,11... | collective-permute-start | bytes 98312 | tf_op jit(solution)/shard_map/ppermute | solution.py:334
  80.4 0.6 copy-start.2
  82.6 11.2 %all-to-all-start.2 = ((bf16[16,24,128]{2,1,0:T(8,128)(2,1)}), bf16[16,24,128]{2,1,0:T(8,128)(2,1)S(1)}, u32[]{:S(2)}, u32[]{:S(2)}) async-start(bf16[16,24,128]{2,1,0:T(8,128)(2,1)} %spread.3), calls=%async_computation.2 | async-start | bytes 196608 | tf_op jit(solution)/shard_map/all_to_all | solution.py:298
  93.8 0.6 copy-start.4
  96.2 1.8 %copy-start.5 = (f32[64,8]{1,0:T(8,128)S(1)}, f32[64,8]{1,0:T(8,128)}, u32[]{:S(2)}) copy-start(f32[64,8]{1,0:T(8,128)} %get-tuple-element.24) | copy-start | bytes 6148

commit v2 on v1

v2 whole, which is shorter than its diff:
```python
import functools
import math
import jax
import jax.numpy as jnp
import numpy as np
from jax import lax
from jax.experimental import pallas as pl
from jax.experimental.pallas import tpu as pltpu
from jax.sharding import Mesh
from jax.sharding import PartitionSpec as P

F32 = jnp.float32
BF16 = jnp.bfloat16
WIRES = (F32, F32, F32)
PINNED = 0
NT = (((1,), (1,)), ((), ()))
NN = (((1,), (0,)), ((), ()))
DEG_OF = [0] + [1] * 3 + [2] * 5 + [3] * 7 + [4] * 9
PACK_ROWS = 144
PAY_ROWS = 384


def dot(a, b, dims=NN):
    return lax.dot_general(a, b, dims, preferred_element_type=F32)


def harmonics(along_x, along_y, along_z):
    sq_x = along_x * along_x
    sq_y = along_y * along_y
    sq_z = along_z * along_z
    root3 = math.sqrt(3.0)
    root15 = math.sqrt(15.0)
    root5 = math.sqrt(5.0)
    coef_a1 = math.sqrt(35.0 / 8.0)
    coef_a2 = math.sqrt(105.0)
    coef_a3 = math.sqrt(21.0 / 8.0)
    coef_a4 = math.sqrt(7.0) / 2.0
    coef_b1 = 3.0 * math.sqrt(35.0) / 2.0
    coef_b2 = 3.0 * math.sqrt(70.0) / 4.0
    coef_b3 = 3.0 * math.sqrt(5.0) / 2.0
    coef_b4 = 3.0 * math.sqrt(10.0) / 4.0
    return [
        jnp.ones_like(along_x),
        root3 * along_y,
        root3 * along_z,
        root3 * along_x,
        root15 * along_x * along_y,
        root15 * along_y * along_z,
        root5 / 2.0 * (3.0 * sq_z - 1.0),
        root15 * along_x * along_z,
        root15 / 2.0 * (sq_x - sq_y),
        coef_a1 * along_y * (3.0 * sq_x - sq_y),
        coef_a2 * along_x * along_y * along_z,
        coef_a3 * along_y * (5.0 * sq_z - 1.0),
        coef_a4 * along_z * (5.0 * sq_z - 3.0),
        coef_a3 * along_x * (5.0 * sq_z - 1.0),
        coef_a2 / 2.0 * along_z * (sq_x - sq_y),
        coef_a1 * along_x * (sq_x - 3.0 * sq_y),
        coef_b1 * along_x * along_y * (sq_x - sq_y),
        coef_b2 * along_y * along_z * (3.0 * sq_x - sq_y),
        coef_b3 * along_x * along_y * (7.0 * sq_z - 1.0),
        coef_b4 * along_y * along_z * (7.0 * sq_z - 3.0),
        0.375 * (35.0 * sq_z * sq_z - 30.0 * sq_z + 3.0),
        coef_b4 * along_x * along_z * (7.0 * sq_z - 3.0),
        coef_b3 / 2.0 * (sq_x - sq_y) * (7.0 * sq_z - 1.0),
        coef_b2 * along_x * along_z * (sq_x - 3.0 * sq_y),
        coef_b1 / 4.0 * (sq_x * (sq_x - 3.0 * sq_y) - sq_y * (3.0 * sq_x - sq_y)),
    ]


def iota(shape, dim):
    return lax.broadcasted_iota(jnp.int32, shape, dim)


VMEM_SPEC = pl.BlockSpec(memory_space=pltpu.VMEM)


def tables_kernel(place_ref, nb_ref, valid_ref, probe_ref, tab_ref):
    slots, probes = nb_ref.shape
    groups = probes // 8
    atoms = place_ref[2]
    idx = nb_ref[...] - place_ref[0]
    idx = jnp.where(idx < 0, idx + atoms, jnp.where(idx >= atoms, idx - atoms, idx))
    idx = idx ^ place_ref[1]
    spot = (iota((probes, 256), 1) // 32) == (iota((probes, 256), 0) & 7)

    def grouped(wide):
        return jnp.sum(jnp.where(spot, wide, 0.0).reshape(groups, 8, 256), axis=1)

    tile = jnp.where((iota((slots, 256), 1) & 31) == iota((slots, 256), 0), 1.0, 0.0).astype(BF16)

    def spread_slots(x):
        return grouped(dot(x.astype(F32).T.astype(BF16), tile))

    tab_ref[0] = 256.0 * spread_slots(idx >> 8) + spread_slots(idx & 255)
    tab_ref[1] = spread_slots(valid_ref[...]) * (1.0 / math.sqrt(slots))
    pos = jnp.concatenate([probe_ref[...].astype(F32), jnp.zeros((5, probes), F32)], axis=0).T
    for i in range(3):
        tab_ref[2 + i] = grouped(jnp.broadcast_to(pos[:, i : i + 1], (probes, 256)))


def tables(place, neighbours, valid, probe_pos):
    groups = neighbours.shape[1] // 8
    return pl.pallas_call(
        tables_kernel,
        out_shape=jax.ShapeDtypeStruct((5, groups, 256), F32),
        in_specs=[pl.BlockSpec(memory_space=pltpu.SMEM)] + [VMEM_SPEC] * 3,
        out_specs=VMEM_SPEC,
        compiler_params=pltpu.CompilerParams(vmem_limit_bytes=8 << 20),
        name="tables",
    )(place, neighbours, valid, probe_pos)


def hot_rows(row, part):
    return jnp.where((iota((256, 256), 0) + 256 * part).astype(F32) == row, 1.0, 0.0).astype(BF16)


def kernel(
    b0, b1, b2, b3, b4, b5, tab_ref, w1t_ref, w2t_ref, ro_ref, cot_ref,
    dens_ref, gf_ref, pay_ref,
    win_ref, feat_ref, pos_ref, sph_ref, rad_ref, w2_ref, cotb_ref, dens_s, gro_s, radial_s,
    hid_ref, slope_ref, bas_ref, gr_ref,
    *, ua, ub, uc, lock,
):
    groups = tab_ref.shape[1]

    def lanes(g):
        return pl.ds(pl.multiple_of(g * 256, 256), 256)

    for i, src in enumerate((b0, b1, b2, b3, b4, b5)):
        win_ref[:, pl.ds(128 * i, 128)] = src[...]
    for l in range(5):
        w2_ref[l] = w2t_ref[:, pl.ds(128 * l, 128)].astype(F32).T.astype(BF16)
    cotb_ref[...] = jnp.broadcast_to(cot_ref[...], (128, 128)).T

    def gather(g, carry):
        row = tab_ref[0, pl.ds(g, 1), :]
        total = None
        for part in range(3):
            piece = dot(win_ref[:, pl.ds(256 * part, 256)], hot_rows(row, part))
            total = piece if total is None else total + piece
        feat_ref[:, lanes(g)] = total[:128].astype(BF16)
        for i in range(3):
            pos_ref[i, pl.ds(g, 1), :] = total[128 + i : 129 + i]
        return carry

    lax.fori_loop(0, groups, gather, 0, unroll=ua)

    idx = tab_ref[0]
    offset = (idx >= 256.0).astype(F32) + (idx >= 512.0).astype(F32) - 1.0
    dx = pos_ref[0] - tab_ref[2]
    dy = pos_ref[1] - tab_ref[3]
    dz = pos_ref[2] + 2.0 * offset - tab_ref[4]
    radius = jnp.sqrt(dx * dx + dy * dy + dz * dz + 0.25)
    rad_ref[...] = radius
    inv = 1.0 / radius
    for k, val in enumerate(harmonics(dx * inv, dy * inv, dz * inv)):
        top = val.astype(BF16).astype(F32)
        sph_ref[0, k] = top
        sph_ref[1, k] = val - top

    gro_s[...] = jnp.zeros_like(gro_s)

    w1 = w1t_ref[...].T
    w1_top = w1.astype(BF16).astype(F32)
    w1_cat = jnp.concatenate([w1_top, w1_top, w1 - w1_top, jnp.zeros_like(w1)], axis=1).astype(BF16)

    def network(g, carry):
        offs = rad_ref[pl.ds(g, 1), :] - 0.75 * iota((8, 256), 0).astype(F32)
        basis = jnp.exp(-2.0 * offs * offs)
        basis_top = basis.astype(BF16).astype(F32)
        basis_cat = jnp.concatenate(
            [basis_top, basis - basis_top, basis_top, jnp.zeros_like(basis)], axis=0
        ).astype(BF16)
        bas_ref[:, lanes(g)] = basis_cat
        preact = dot(w1_cat, basis_cat)
        sig = 1.0 / (1.0 + jnp.exp(-preact))
        hid_ref[:, lanes(g)] = (preact * sig).astype(BF16)
        slope_ref[:, lanes(g)] = sig * (1.0 + preact * (1.0 - sig))
        return carry

    lax.fori_loop(0, groups, network, 0, unroll=ub)

    mask = iota((8, 256), 0) == iota((8, 256), 1) // 32

    def spheres(g):
        tops, lows = [], []
        for l in range(5):
            for half, out in ((0, tops), (1, lows)):
                rows = [
                    jnp.where(mask, sph_ref[half, k, pl.ds(g, 1), :], 0.0)
                    for k in range(l * l, (l + 1) * (l + 1))
                ]
                out.append(jnp.concatenate(rows, axis=0) if len(rows) > 1 else rows[0])
        return tops, lows

    def forward(g, u, sph):
        tops, lows = sph
        fw = feat_ref[:, lanes(g)].astype(F32) * tab_ref[1, pl.ds(g, 1), :]
        hidden = hid_ref[:, lanes(g)]
        msgs = []
        for l in range(5):
            radial = dot(w2_ref[l], hidden)
            radial_s[u, l] = radial
            msgs.append((radial * fw).astype(BF16))
        moms = []
        for degs in ((0, 1), (2, 3), (4,)):
            rows = jnp.concatenate([x for l in degs for x in (tops[l], lows[l])], axis=0).astype(BF16)
            right = jnp.concatenate([msgs[l] for l in degs], axis=0) if len(degs) > 1 else msgs[degs[0]]
            out = dot(rows, right, NT)
            at = 0
            for i, l in enumerate(degs):
                size = 8 * (2 * l + 1)
                cols = slice(128 * i, 128 * i + 128)
                moms.append(out[at : at + size, cols] + out[at + size : at + 2 * size, cols])
                at += 2 * size
        return moms

    def middle(g, moms):
        cot = cotb_ref[pl.ds(pl.multiple_of(g * 8, 8), 8), :]
        dens = None
        grads = []
        for l, mom in enumerate(moms):
            ro = ro_ref[pl.ds(l, 1), :]
            parts = [mom[8 * i : 8 * i + 8] for i in range(2 * l + 1)]
            if l == 0:
                squares = parts[0]
                grads.append(cot * ro)
            else:
                squares = None
                for x in parts:
                    squares = x * x if squares is None else squares + x * x
                fac = 2.0 * cot * ro
                grads.append(jnp.concatenate([x * fac for x in parts], axis=0))
            dens = squares * ro if dens is None else dens + squares * ro
            gro_s[l] += squares * cot
        dens_s[pl.ds(pl.multiple_of(g * 8, 8), 8), :] = dens
        return grads

    def backward(g, u, sph, grads):
        tops, lows = sph
        wgt = tab_ref[1, pl.ds(g, 1), :]
        fw = feat_ref[:, lanes(g)].astype(F32) * wgt
        gf = None
        for l in range(5):
            top = grads[l].astype(BF16).astype(F32)
            left = jnp.concatenate([top, top, grads[l] - top], axis=0).T.astype(BF16)
            right = jnp.concatenate([tops[l], lows[l], tops[l]], axis=0).astype(BF16)
            gmsg = dot(left, right)
            piece = gmsg * radial_s[u, l]
            gf = piece if gf is None else gf + piece
            gr_ref[pl.ds(128 * l, 128), lanes(g)] = (gmsg * fw).astype(BF16)
        gf_ref[:, lanes(g)] = (gf * wgt).astype(BF16)

    def block(i, carry):
        gs = [i * lock + u for u in range(lock)]
        sphs = [spheres(g) for g in gs]
        moms = [forward(g, u, sphs[u]) for u, g in enumerate(gs)]
        grads = [middle(g, moms[u]) for u, g in enumerate(gs)]
        for u, g in enumerate(gs):
            backward(g, u, sphs[u], grads[u])
        return carry

    lax.fori_loop(0, groups // lock, block, 0, unroll=uc)

    hid = hid_ref[...]
    gr = gr_ref[...]
    for l in range(5):
        pay_ref[pl.ds(64 * l, 64), :] = dot(hid, gr_ref[pl.ds(128 * l, 128), :], NT).astype(pay_ref.dtype)
    gpre = (dot(w2t_ref[...], gr) * slope_ref[...]).astype(BF16)
    gw1 = dot(bas_ref[...], gpre, NT)
    gw1 = gw1[:8, :] + gw1[8:16, :]
    gw1 = jnp.concatenate([gw1, jnp.zeros((8, 64), F32)], axis=1)
    gro = jnp.concatenate(
        [jnp.sum(gro_s[l], axis=0, keepdims=True) for l in range(5)] + [jnp.zeros((3, 128), F32)], axis=0
    )
    pay_ref[pl.ds(320, 16), :] = jnp.concatenate([gro, gw1], axis=0).astype(pay_ref.dtype)
    pay_ref[pl.ds(336, 48), :] = jnp.zeros((48, 128), pay_ref.dtype)
    dens_ref[...] = lax.dot_general(
        jnp.ones((8, 128), F32), dens_s[...], NT, precision=lax.Precision.HIGHEST, preferred_element_type=F32
    )


def scatter_kernel(gf_ref, tab_ref, *outs):
    groups = tab_ref.shape[1]
    for part in range(3):
        total = None
        for g in range(groups):
            row = tab_ref[0, pl.ds(g, 1), :]
            piece = dot(gf_ref[:, pl.ds(256 * g, 256)], hot_rows(row, part), NT)
            total = piece if total is None else total + piece
        total = total.astype(BF16)
        outs[part][:128] = total[:, :128]
        outs[part][128:] = total[:, 128:]


def scatter(gf, tab):
    return pl.pallas_call(
        scatter_kernel,
        out_shape=(jax.ShapeDtypeStruct((256, 128), BF16),) * 3,
        in_specs=[VMEM_SPEC] * 2,
        out_specs=[VMEM_SPEC] * 3,
        compiler_params=pltpu.CompilerParams(vmem_limit_bytes=16 << 20),
        name="scatter_feat",
    )(gf, tab)


def layer(blocks, tab, w1t, w2t, ro, cot, ua=8, ub=8, uc=1, lock=4):
    groups = tab.shape[1]
    edges = groups * 256
    return pl.pallas_call(
        functools.partial(kernel, ua=ua, ub=ub, uc=uc, lock=lock),
        out_shape=(
            jax.ShapeDtypeStruct((8, 128), F32),
            jax.ShapeDtypeStruct((128, edges), BF16),
            jax.ShapeDtypeStruct((PAY_ROWS, 128), WIRES[0]),
        ),
        in_specs=[VMEM_SPEC] * 11,
        out_specs=[VMEM_SPEC] * 3,
        scratch_shapes=[
            pltpu.VMEM((PACK_ROWS, 768), BF16),
            pltpu.VMEM((128, edges), BF16),
            pltpu.VMEM((3, groups, 256), F32),
            pltpu.VMEM((2, 25, groups, 256), F32),
            pltpu.VMEM((groups, 256), F32),
            pltpu.VMEM((5, 128, 64), BF16),
            pltpu.VMEM((128, 128), F32),
            pltpu.VMEM((128, 128), F32),
            pltpu.VMEM((5, 8, 128), F32),
            pltpu.VMEM((lock, 5, 128, 256), F32),
            pltpu.VMEM((64, edges), BF16),
            pltpu.VMEM((64, edges), F32),
            pltpu.VMEM((32, edges), BF16),
            pltpu.VMEM((640, edges), BF16),
        ],
        compiler_params=pltpu.CompilerParams(vmem_limit_bytes=32 << 20),
        name="probe_layer",
    )(*blocks, tab, w1t, w2t, ro, cot)


def finish_kernel(scale, x_ref, w1_ref, w2_ref, ro_ref):
    for l in range(5):
        w2_ref[:, pl.ds(128 * l, 128)] = x_ref[pl.ds(64 * l, 64), :] * scale
    ro_ref[...] = x_ref[pl.ds(320, 8), :][:5] * scale
    w1_ref[...] = x_ref[pl.ds(328, 8), :][:, :64] * scale


def finish(x, scale):
    return pl.pallas_call(
        functools.partial(finish_kernel, scale),
        out_shape=(
            jax.ShapeDtypeStruct((8, 64), F32),
            jax.ShapeDtypeStruct((64, 640), F32),
            jax.ShapeDtypeStruct((5, 128), F32),
        ),
        in_specs=[VMEM_SPEC],
        out_specs=[VMEM_SPEC] * 3,
        compiler_params=pltpu.CompilerParams(vmem_limit_bytes=8 << 20),
        name="finish",
    )(x)


AXES = ("z", "ylo", "x", "core", "yhi")
SLAB = ("z", "ylo", "x", "core")
NEAR = ("ylo", "x", "core")
FAR = ("z", "yhi")


def exchange(x, axes):
    return lax.all_to_all(x, axes, 0, 0, tiled=True)


def passed_along(block, distance):
    count = lax.axis_size(SLAB)
    return lax.ppermute(block, SLAB, [(i, (i + distance) % count) for i in range(count)])


def sent(block, slab_step, plane_step):
    slabs, planes = lax.axis_size(SLAB), lax.axis_size("yhi")
    route = [
        (s * planes + p, (s + slab_step) % slabs * planes + (p + plane_step) % planes)
        for s in range(slabs)
        for p in range(planes)
    ]
    return lax.ppermute(block, AXES, route)


def joined(mine, other):
    even = lax.axis_index("yhi") == 0
    return jnp.concatenate([jnp.where(even, mine, other), jnp.where(even, other, mine)], axis=1)


def totals(x, copies, wire):
    total = jnp.sum(x.astype(F32), axis=0).astype(wire)
    return jnp.broadcast_to(total[None], (copies,) + total.shape)


def shards(probe_pos, atom_pos, atom_feat, neighbours, valid, w_radial1, w_radial2, readout, cotangent):
    slab_count = lax.axis_size(SLAB)
    slab_index = lax.axis_index(SLAB)
    planes = lax.axis_size("yhi")
    plane = lax.axis_index("yhi")
    atom_dev = atom_feat.shape[1]
    atom_slab = atom_dev * planes
    pack = jnp.concatenate(
        [atom_feat, atom_pos, jnp.zeros((PACK_ROWS - 131, atom_dev), BF16)], axis=0
    )
    steps = ((-1, 0), (-1, 1), (0, 0), (0, 1), (1, 0), (1, 1))
    blocks = [pack if step == (0, 0) else sent(pack, -step[0], step[1]) for step in steps]
    place = jnp.stack(
        [(slab_index - 1) * atom_slab, plane * atom_dev, jnp.full((), slab_count * atom_slab, jnp.int32)]
    )
    tab = tables(place, neighbours, valid, probe_pos)
    dens, edge_grad, pay = layer(
        blocks, tab, w_radial1.T, w_radial2.T, readout, cotangent.reshape(1, -1)
    )
    density = dens[0]
    near, far = lax.axis_size(NEAR), lax.axis_size(FAR)
    part = exchange(pay.reshape(near, PAY_ROWS // near, 128).astype(WIRES[0]), NEAR)
    to_low, own_grad, to_high = scatter(edge_grad, tab)
    wide = totals(part, far, WIRES[1])
    if PINNED:
        wide, to_low, to_high = lax.optimization_barrier((wide, to_low, to_high))
    part = exchange(wide, FAR)
    from_high = passed_along(to_low, -1)
    from_low = passed_along(to_high, 1)
    slab_sum = own_grad.astype(F32) + from_high.astype(F32) + from_low.astype(F32)
    wide = totals(part, near, WIRES[2])
    other = slab_sum[atom_dev:].astype(BF16)
    if PINNED > 1:
        wide, other = lax.optimization_barrier((wide, other))
    part = exchange(wide, NEAR)
    grad_feat = slab_sum[:atom_dev] + sent(other, 0, 1).astype(F32)
    scale = 1.0 / math.sqrt(neighbours.shape[1] * slab_count * planes)
    w1t, w2t, grad_ro = finish(part.reshape(PAY_ROWS, 128), scale)
    grad_w1, grad_w2 = w1t.T, w2t.T
    return density, grad_feat, grad_w1, grad_w2, grad_ro


def solution(mesh):
    fine = Mesh(np.asarray(mesh.devices).reshape(8, 2, 4, 2, 2), AXES)
    flat = P(None, AXES)
    in_specs = (flat, flat, flat, flat, flat, P(), P(), P(), P(AXES))
    out_specs = (P(AXES), flat, P(), P(), P())
    return jax.shard_map(shards, mesh=fine, in_specs=in_specs, out_specs=out_specs, check_vma=False)
```

time: 99.4 us -> 79.2 us (0.80)
  Pallas kernels: 31.4 us -> 16.7 us
  local copies, waits for them, and re-layouts: 11.3 us -> 3.84 us
  blocking collectives: 5.77 us -> 0 us
  waiting for transfers between devices: 15.4 us -> 20.4 us
  starting transfers between devices: 32.1 us -> 35.3 us
    pallas_call x3, Pallas kernels: 29.6 us -> 16 us  [the longest x1 12.9 us: layer(): pl.pallas_call(functools.partial(kernel, ua=ua, ub=ub, uc=uc, lock=lock),...]
    ppermute x1 -> x6, starting transfers between devices: 2.95 us -> 14.8 us  [sent(): return lax.ppermute(block, AXES, route)]
    unnamed x30 -> x16, local copies, waits for them, and re-layouts: 9.49 us -> 1.87 us
    all_gather x1 -> x0, blocking collectives: 5.77 us -> none  [shards(): own = lax.all_gather(pack, 'yhi', axis=1, tiled=True)]
    all_to_all x3, starting transfers between devices: 23.7 us -> 18.6 us  [exchange(): return lax.all_to_all(x, axes, 0, 0, tiled=True)]
    ppermute x1 -> x6, waiting for transfers between devices: 0.01 us -> 4.17 us  [sent(): return lax.ppermute(block, AXES, route)]
    ppermute x4 -> x2, starting transfers between devices: 5.42 us -> 1.82 us  [passed_along(): lax.ppermute(block, SLAB, [(i, (i + distance) % count) for i in range(cou...]
    broadcast_in_dim x2, local copies, waits for them, and re-layouts: 0.19 us -> 1.37 us  [totals(): return jnp.broadcast_to(total[None], (copies,) + total.shape)]
  transfers between devices with their start and end apart: 8 -> 11, of which waited for: 3 -> 5; matrix products, arithmetic and copies ran while one was open for 3% -> 3% of each run, Pallas kernels for 3% -> 4%
where the time goes in v2:
time: 79.2 us; the launch traced here: 78.6 us
  starting transfers between devices  35.3 us (45%)
  waiting for transfers between devices  20.4 us (26%)
  Pallas kernels  16.7 us (21%)
  local copies, waits for them, and re-layouts  3.84 us (5%)
  other arithmetic  1.62 us (2%)
  between operations  0.81 us (1%)
    all_to_all x3, starting transfers between devices, exchange(): return lax.all_to_all(x, axes, 0, 0, tiled=True)  18.6 us
    all_to_all x3, waiting for transfers between devices, exchange(): return lax.all_to_all(x, axes, 0, 0, tiled=True)  16.2 us
    ppermute x6, starting transfers between devices, sent(): return lax.ppermute(block, AXES, route)  14.8 us
    pallas_call x1, Pallas kernels, layer(): pl.pallas_call(functools.partial(kernel, ua=ua, ub=ub, uc=uc, lock=lock),...  12.9 us
    ppermute x6, waiting for transfers between devices, sent(): return lax.ppermute(block, AXES, route)  4.17 us
    pallas_call x1, Pallas kernels, scatter(): pl.pallas_call(scatter_kernel, out_shape=(jax.ShapeDtypeStruct((256, 128)...  2.17 us
    unnamed x16, local copies, waits for them, and re-layouts  1.87 us
    ppermute x2, starting transfers between devices, passed_along(): lax.ppermute(block, SLAB, [(i, (i + distance) % count) for i in range(cou...  1.82 us
  transfers between devices with their start and end apart: 11, of which 5 were waited for; matrix products, arithmetic and copies ran while one was open for 3% of the time, Pallas kernels for 4%

profile of v2, /device:TPU:1, one launch (start us, length us, event | category | flops | bytes accessed | tf_op | source)
XLA Modules:
  0.0 78.6 jit_solution(9186455757415634675)
XLA Ops:
  0.6 0.0 copy-start.7
  0.7 0.1 pad.5.clone
  0.7 0.6 copy-done.7
  1.3 0.8 %maximum_maximum_fusion.b2 = bf16[144,128]{1,0:T(8,128)(2,1)S(1)} fusion(bf16[3,128]{1,0:T(4,128)(2,1)S(1)} %copy-done.7, bf16[128,128]{1,0:T(8,128)(2,1)} %param.11, bf16[144]{0:T(256)(128)(2,1)S(1)} %pad.5.clone), kind=kLoop, calls=%fused_computation.3 | loop fusion | flops 110592 | bytes 70688 | tf_op jit(solution)/shard_map/concatenate | solution.py:405
  2.2 4.4 %collective-permute-start.4 = (bf16[144,128]{1,0:T(8,128)(2,1)S(1)}, bf16[144,128]{1,0:T(8,128)(2,1)S(1)}, u32[]{:S(2)}, u32[]{:S(2)}) collective-permute-start(bf16[144,128]{1,0:T(8,128)(2,1)S(1)} %maximum_maximum_fusion.b2), channel_id=1, source_target_pairs={{0,255},{1,254},{2,1},{3,0},{4,3},{5,2},{6,5},{7,4},{8,7},{9,6},{1... | collective-permute-start | bytes 110600 | tf_op jit(solution)/shard_map/ppermute | solution.py:385
  6.5 7.1 %collective-permute-start.3 = (bf16[144,128]{1,0:T(8,128)(2,1)S(1)}, bf16[144,128]{1,0:T(8,128)(2,1)S(1)}, u32[]{:S(2)}, u32[]{:S(2)}) collective-permute-start(bf16[144,128]{1,0:T(8,128)(2,1)S(1)} %maximum_maximum_fusion.b2), channel_id=1, source_target_pairs={{0,254},{1,255},{2,0},{3,1},{4,2},{5,3},{6,4},{7,5},{8,6},{9,7},{1... | collective-permute-start | bytes 110600 | tf_op jit(solution)/shard_map/ppermute | solution.py:385
  13.7 0.4 collective-permute-start.2
  14.0 0.0 copy-start.2
  14.1 0.0 copy-start
  14.1 0.1 pad_add_fusion.place_ref
  14.2 0.6 copy-done.1
  14.8 0.0 copy-done.2
  14.8 1.0 %tables.1.tab_ref = f32[5,16,256]{2,1,0:T(8,128)S(1)} custom-call(s32[3]{0:T(128)S(1)} %pad_add_fusion.place_ref, s32[32,128]{1,0:T(8,128)S(1)} %copy-done.1, s32[32,128]{1,0:T(8,128)S(1)} %copy-done.2, bf16[3,128]{1,0:T(4,128)(2,1)S(1)} %copy-done.5), custom_call_target="tpu_custom_call" | custom-call | tf_op jit(solution)/shard_map/tables/pallas_call | solution.py:104
  15.8 2.4 %collective-permute-done.2.b3 = bf16[144,128]{1,0:T(8,128)(2,1)S(1)} collective-permute-done((bf16[144,128]{1,0:T(8,128)(2,1)S(1)}, bf16[144,128]{1,0:T(8,128)(2,1)S(1)}, u32[]{:S(2)}, u32[]{:S(2)}) %collective-permute-start.2) | collective-permute-done | bytes 36896 | tf_op jit(solution)/shard_map/ppermute | solution.py:385
  18.2 1.8 %collective-permute-done.1.b1 = bf16[144,128]{1,0:T(8,128)(2,1)S(1)} collective-permute-done((bf16[144,128]{1,0:T(8,128)(2,1)S(1)}, bf16[144,128]{1,0:T(8,128)(2,1)S(1)}, u32[]{:S(2)}, u32[]{:S(2)}) %collective-permute-start.1) | collective-permute-done | bytes 36896 | tf_op jit(solution)/shard_map/ppermute | solution.py:385
  20.0 0.6 copy-done.6
  20.6 12.9 %probe_layer.1 = (f32[8,128]{1,0:T(8,128)S(1)}, bf16[128,4096]{1,0:T(8,128)(2,1)S(1)}, f32[384,128]{1,0:T(8,128)}) custom-call(bf16[144,128]{1,0:T(8,128)(2,1)S(1)} %collective-permute-done.b0, bf16[144,128]{1,0:T(8,128)(2,1)S(1)} %collective-permute-done.1.b1, bf16[144,128]{1,0:T(8,128)(2,1)S(1)} %maximum_maximum_fusion.b2, ...), custom_call_target="tpu_custom_call" | custom-call | tf_op jit(solution)/shard_map/probe_layer/pallas_call | solution.py:311
  33.5 8.8 %all-to-all-start = ((f32[16,24,128]{2,1,0:T(8,128)}), f32[16,24,128]{2,1,0:T(8,128)S(1)}, u32[]{:S(2)}, u32[]{:S(2)}) async-start(f32[16,24,128]{2,1,0:T(8,128)} %bitcast.6), calls=%async_computation | async-start | bytes 393216 | tf_op jit(solution)/shard_map/all_to_all | solution.py:370
  42.3 2.2 %scatter_feat.1 = (bf16[256,128]{1,0:T(8,128)(2,1)S(1)}, bf16[256,128]{1,0:T(8,128)(2,1)S(1)}, bf16[256,128]{1,0:T(8,128)(2,1)S(1)}) custom-call(bf16[128,4096]{1,0:T(8,128)(2,1)S(1)} %get-tuple-element.15.gf_ref, f32[5,16,256]{2,1,0:T(8,128)S(1)} %tables.1.tab_ref), custom_call_target="tpu_custom_call" | custom-call | tf_op jit(solution)/shard_map/scatter_feat/pallas_call | solution.py:298
  44.5 0.3 collective-permute-start.5
  44.8 1.5 %collective-permute-start.6 = (bf16[256,128]{1,0:T(8,128)(2,1)S(1)}, bf16[256,128]{1,0:T(8,128)(2,1)S(1)}, u32[]{:S(2)}, u32[]{:S(2)}) collective-permute-start(bf16[256,128]{1,0:T(8,128)(2,1)S(1)} %get-tuple-element.18), channel_id=1, source_target_pairs={{0,2},{2,4},{4,6},{6,8},{8,10},{10,12},{12,14},{14,16},{16,18},{18... | collective-permute-start | bytes 196616 | tf_op jit(solution)/shard_map/ppermute | solution.py:375
  46.3 2.7 %all-to-all-done = f32[16,24,128]{2,1,0:T(8,128)S(1)} async-done(((f32[16,24,128]{2,1,0:T(8,128)}), f32[16,24,128]{2,1,0:T(8,128)S(1)}, u32[]{:S(2)}, u32[]{:S(2)}) %all-to-all-start) | async-done | bytes 196640 | tf_op jit(solution)/shard_map/all_to_all | solution.py:370
  49.0 0.7 broadcast_in_dim.7
  49.7 3.8 %all-to-all-start.1 = ((f32[16,24,128]{2,1,0:T(8,128)}), f32[16,24,128]{2,1,0:T(8,128)S(1)}, u32[]{:S(2)}, u32[]{:S(2)}) async-start(f32[16,24,128]{2,1,0:T(8,128)} %broadcast_in_dim.7), calls=%async_computation.1 | async-start | bytes 393216 | tf_op jit(solution)/shard_map/all_to_all | solution.py:370
  53.6 3.0 %collective-permute-start.7 = (bf16[128,128]{1,0:T(8,128)(2,1)S(1)}, bf16[128,128]{1,0:T(8,128)(2,1)S(1)}, u32[]{:S(2)}, u32[]{:S(2)}) collective-permute-start(bf16[128,128]{1,0:T(8,128)(2,1)S(1)} %slice.18), channel_id=1, source_target_pairs={{0,1},{1,0},{2,3},{3,2},{4,5},{5,4},{6,7},{7,6},{8,9},{9,8},{10,11... | collective-permute-start | bytes 98312 | tf_op jit(solution)/shard_map/ppermute | solution.py:385
  56.6 0.5 slice_bitcast_fusion
  57.1 7.5 %all-to-all-done.1 = f32[16,24,128]{2,1,0:T(8,128)S(1)} async-done(((f32[16,24,128]{2,1,0:T(8,128)}), f32[16,24,128]{2,1,0:T(8,128)S(1)}, u32[]{:S(2)}, u32[]{:S(2)}) %all-to-all-start.1) | async-done | bytes 196640 | tf_op jit(solution)/shard_map/all_to_all | solution.py:370
  64.6 0.7 broadcast_in_dim.8
  65.3 6.0 %all-to-all-start.2 = ((f32[16,24,128]{2,1,0:T(8,128)}), f32[16,24,128]{2,1,0:T(8,128)S(1)}, u32[]{:S(2)}, u32[]{:S(2)}) async-start(f32[16,24,128]{2,1,0:T(8,128)} %broadcast_in_dim.8), calls=%async_computation.2 | async-start | bytes 393216 | tf_op jit(solution)/shard_map/all_to_all | solution.py:370
  71.3 0.6 slice_add_fusion
  72.0 6.0 %all-to-all-done.2 = f32[16,24,128]{2,1,0:T(8,128)S(1)} async-done(((f32[16,24,128]{2,1,0:T(8,128)}), f32[16,24,128]{2,1,0:T(8,128)S(1)}, u32[]{:S(2)}, u32[]{:S(2)}) %all-to-all-start.2) | async-done | bytes 196640 | tf_op jit(solution)/shard_map/all_to_all | solution.py:370
  78.0 0.7 finish.1
  (22 shorter events, 0.1 us)
Async XLA Ops:
  0.6 0.7 copy-start.7
  2.2 13.6 %collective-permute-start.4 = (bf16[144,128]{1,0:T(8,128)(2,1)S(1)}, bf16[144,128]{1,0:T(8,128)(2,1)S(1)}, u32[]{:S(2)}, u32[]{:S(2)}) collective-permute-start(bf16[144,128]{1,0:T(8,128)(2,1)S(1)} %maximum_maximum_fusion.b2), channel_id=1, source_target_pairs={{0,255},{1,254},{2,1},{3,0},{4,3},{5,2},{6,5},{7,4},{8,7},{9,6},{1... | collective-permute-start | bytes 110600 | tf_op jit(solution)/shard_map/ppermute | solution.py:385
  6.5 9.3 %collective-permute-start.3 = (bf16[144,128]{1,0:T(8,128)(2,1)S(1)}, bf16[144,128]{1,0:T(8,128)(2,1)S(1)}, u32[]{:S(2)}, u32[]{:S(2)}) collective-permute-start(bf16[144,128]{1,0:T(8,128)(2,1)S(1)} %maximum_maximum_fusion.b2), channel_id=1, source_target_pairs={{0,254},{1,255},{2,0},{3,1},{4,2},{5,3},{6,4},{7,5},{8,6},{9,7},{1... | collective-permute-start | bytes 110600 | tf_op jit(solution)/shard_map/ppermute | solution.py:385
  13.7 4.5 %collective-permute-start.2 = (bf16[144,128]{1,0:T(8,128)(2,1)S(1)}, bf16[144,128]{1,0:T(8,128)(2,1)S(1)}, u32[]{:S(2)}, u32[]{:S(2)}) collective-permute-start(bf16[144,128]{1,0:T(8,128)(2,1)S(1)} %maximum_maximum_fusion.b2), channel_id=1, source_target_pairs={{0,1},{1,0},{2,3},{3,2},{4,5},{5,4},{6,7},{7,6},{8,9},{9,8},{10,11... | collective-permute-start | bytes 110600 | tf_op jit(solution)/shard_map/ppermute | solution.py:385
  14.0 6.0 %collective-permute-start.1 = (bf16[144,128]{1,0:T(8,128)(2,1)S(1)}, bf16[144,128]{1,0:T(8,128)(2,1)S(1)}, u32[]{:S(2)}, u32[]{:S(2)}) collective-permute-start(bf16[144,128]{1,0:T(8,128)(2,1)S(1)} %maximum_maximum_fusion.b2), channel_id=1, source_target_pairs={{0,3},{1,2},{2,5},{3,4},{4,7},{5,6},{6,9},{7,8},{8,11},{9,10},{10,... | collective-permute-start | bytes 110600 | tf_op jit(solution)/shard_map/ppermute | solution.py:385
  14.0 6.0 %collective-permute-start = (bf16[144,128]{1,0:T(8,128)(2,1)S(1)}, bf16[144,128]{1,0:T(8,128)(2,1)S(1)}, u32[]{:S(2)}, u32[]{:S(2)}) collective-permute-start(bf16[144,128]{1,0:T(8,128)(2,1)S(1)} %maximum_maximum_fusion.b2), channel_id=1, source_target_pairs={{0,2},{1,3},{2,4},{3,5},{4,6},{5,7},{6,8},{7,9},{8,10},{9,11},{10,... | collective-permute-start | bytes 110600 | tf_op jit(solution)/shard_map/ppermute | solution.py:385
  14.0 0.7 copy-start.1
  14.0 0.7 copy-start.2
  14.1 0.7 copy-start.5
  14.1 5.9 %copy-start = (bf16[640,64]{0,1:T(8,128)(2,1)S(1)}, bf16[640,64]{0,1:T(8,128)(2,1)}, u32[]{:S(2)}) copy-start(bf16[640,64]{0,1:T(8,128)(2,1)} %param.15) | copy-start | bytes 245764
  14.8 5.2 %copy-start.4 = (f32[5,128]{1,0:T(8,128)S(1)}, f32[5,128]{1,0:T(8,128)}, u32[]{:S(2)}) copy-start(f32[5,128]{1,0:T(8,128)} %ro_ref.1) | copy-start | bytes 7684
  15.8 4.2 %copy-start.3 = (f32[64,8]{0,1:T(8,128)S(1)}, f32[64,8]{0,1:T(8,128)}, u32[]{:S(2)}) copy-start(f32[64,8]{0,1:T(8,128)} %param.14) | copy-start | bytes 6148
  20.0 0.7 copy-start.6
  33.5 15.5 %all-to-all-start = ((f32[16,24,128]{2,1,0:T(8,128)}), f32[16,24,128]{2,1,0:T(8,128)S(1)}, u32[]{:S(2)}, u32[]{:S(2)}) async-start(f32[16,24,128]{2,1,0:T(8,128)} %bitcast.6), calls=%async_computation | async-start | bytes 393216 | tf_op jit(solution)/shard_map/all_to_all | solution.py:370
  44.5 9.1 %collective-permute-start.5 = (bf16[256,128]{1,0:T(8,128)(2,1)S(1)}, bf16[256,128]{1,0:T(8,128)(2,1)S(1)}, u32[]{:S(2)}, u32[]{:S(2)}) collective-permute-start(bf16[256,128]{1,0:T(8,128)(2,1)S(1)} %get-tuple-element.17), channel_id=1, source_target_pairs={{0,254},{2,0},{4,2},{6,4},{8,6},{10,8},{12,10},{14,12},{16,14},{18... | collective-permute-start | bytes 196616 | tf_op jit(solution)/shard_map/ppermute | solution.py:375
  44.8 8.8 %collective-permute-start.6 = (bf16[256,128]{1,0:T(8,128)(2,1)S(1)}, bf16[256,128]{1,0:T(8,128)(2,1)S(1)}, u32[]{:S(2)}, u32[]{:S(2)}) collective-permute-start(bf16[256,128]{1,0:T(8,128)(2,1)S(1)} %get-tuple-element.18), channel_id=1, source_target_pairs={{0,2},{2,4},{4,6},{6,8},{8,10},{10,12},{12,14},{14,16},{16,18},{18... | collective-permute-start | bytes 196616 | tf_op jit(solution)/shard_map/ppermute | solution.py:375
  49.7 14.9 %all-to-all-start.1 = ((f32[16,24,128]{2,1,0:T(8,128)}), f32[16,24,128]{2,1,0:T(8,128)S(1)}, u32[]{:S(2)}, u32[]{:S(2)}) async-start(f32[16,24,128]{2,1,0:T(8,128)} %broadcast_in_dim.7), calls=%async_computation.1 | async-start | bytes 393216 | tf_op jit(solution)/shard_map/all_to_all | solution.py:370
  53.6 17.7 %collective-permute-start.7 = (bf16[128,128]{1,0:T(8,128)(2,1)S(1)}, bf16[128,128]{1,0:T(8,128)(2,1)S(1)}, u32[]{:S(2)}, u32[]{:S(2)}) collective-permute-start(bf16[128,128]{1,0:T(8,128)(2,1)S(1)} %slice.18), channel_id=1, source_target_pairs={{0,1},{1,0},{2,3},{3,2},{4,5},{5,4},{6,7},{7,6},{8,9},{9,8},{10,11... | collective-permute-start | bytes 98312 | tf_op jit(solution)/shard_map/ppermute | solution.py:385
  65.3 12.6 %all-to-all-start.2 = ((f32[16,24,128]{2,1,0:T(8,128)}), f32[16,24,128]{2,1,0:T(8,128)S(1)}, u32[]{:S(2)}, u32[]{:S(2)}) async-start(f32[16,24,128]{2,1,0:T(8,128)} %broadcast_in_dim.8), calls=%async_computation.2 | async-start | bytes 393216 | tf_op jit(solution)/shard_map/all_to_all | solution.py:370

commit v3 on v2

--- a/solution.py
+++ b/solution.py
@@ -75,7 +75,8 @@
 VMEM_SPEC = pl.BlockSpec(memory_space=pltpu.VMEM)
 
 
-def tables_kernel(place_ref, nb_ref, valid_ref, probe_ref, tab_ref):
+def tables_kernel(place_ref, nb_ref, valid_ref, probe_ref, cot_ref, tab_ref, cotb_ref):
+    cotb_ref[...] = jnp.broadcast_to(cot_ref[...], (128, 128)).T
     slots, probes = nb_ref.shape
     groups = probes // 8
     atoms = place_ref[2]
@@ -99,16 +100,16 @@
         tab_ref[2 + i] = grouped(jnp.broadcast_to(pos[:, i : i + 1], (probes, 256)))
 
 
-def tables(place, neighbours, valid, probe_pos):
+def tables(place, neighbours, valid, probe_pos, cotangent):
     groups = neighbours.shape[1] // 8
     return pl.pallas_call(
         tables_kernel,
-        out_shape=jax.ShapeDtypeStruct((5, groups, 256), F32),
-        in_specs=[pl.BlockSpec(memory_space=pltpu.SMEM)] + [VMEM_SPEC] * 3,
-        out_specs=VMEM_SPEC,
+        out_shape=(jax.ShapeDtypeStruct((5, groups, 256), F32), jax.ShapeDtypeStruct((128, 128), F32)),
+        in_specs=[pl.BlockSpec(memory_space=pltpu.SMEM)] + [VMEM_SPEC] * 4,
+        out_specs=[VMEM_SPEC] * 2,
         compiler_params=pltpu.CompilerParams(vmem_limit_bytes=8 << 20),
         name="tables",
-    )(place, neighbours, valid, probe_pos)
+    )(place, neighbours, valid, probe_pos, cotangent)
 
 
 def hot_rows(row, part):
@@ -116,9 +117,9 @@
 
 
 def kernel(
-    b0, b1, b2, b3, b4, b5, tab_ref, w1t_ref, w2t_ref, ro_ref, cot_ref,
+    b0, b1, b2, b3, b4, b5, tab_ref, w1t_ref, w2t_ref, ro_ref, cotb_ref,
     dens_ref, gf_ref, pay_ref,
-    win_ref, feat_ref, pos_ref, sph_ref, rad_ref, w2_ref, cotb_ref, dens_s, gro_s, radial_s,
+    win_ref, feat_ref, pos_ref, sph_ref, rad_ref, w2_ref, dens_s, gro_s, radial_s,
     hid_ref, slope_ref, bas_ref, gr_ref,
     *, ua, ub, uc, lock,
 ):
@@ -131,7 +132,6 @@
         win_ref[:, pl.ds(128 * i, 128)] = src[...]
     for l in range(5):
         w2_ref[l] = w2t_ref[:, pl.ds(128 * l, 128)].astype(F32).T.astype(BF16)
-    cotb_ref[...] = jnp.broadcast_to(cot_ref[...], (128, 128)).T
 
     def gather(g, carry):
         row = tab_ref[0, pl.ds(g, 1), :]
@@ -305,7 +305,7 @@
     )(gf, tab)
 
 
-def layer(blocks, tab, w1t, w2t, ro, cot, ua=8, ub=8, uc=1, lock=4):
+def layer(blocks, tab, w1t, w2t, ro, cot, ua=16, ub=16, uc=1, lock=4):
     groups = tab.shape[1]
     edges = groups * 256
     return pl.pallas_call(
@@ -325,7 +325,6 @@
             pltpu.VMEM((groups, 256), F32),
             pltpu.VMEM((5, 128, 64), BF16),
             pltpu.VMEM((128, 128), F32),
-            pltpu.VMEM((128, 128), F32),
             pltpu.VMEM((5, 8, 128), F32),
             pltpu.VMEM((lock, 5, 128, 256), F32),
             pltpu.VMEM((64, edges), BF16),
@@ -410,9 +409,9 @@
     place = jnp.stack(
         [(slab_index - 1) * atom_slab, plane * atom_dev, jnp.full((), slab_count * atom_slab, jnp.int32)]
     )
-    tab = tables(place, neighbours, valid, probe_pos)
+    tab, cot = tables(place, neighbours, valid, probe_pos, cotangent.reshape(1, -1))
     dens, edge_grad, pay = layer(
-        blocks, tab, w_radial1.T, w_radial2.T, readout, cotangent.reshape(1, -1)
+        blocks, tab, w_radial1.T, w_radial2.T, readout, cot
     )
     density = dens[0]
     near, far = lax.axis_size(NEAR), lax.axis_size(FAR)

time: 79.2 us -> 77.9 us (0.984)
  no operation moved by 1% of the time
where the time goes in v3:
time: 77.9 us; the launch traced here: 77.4 us
  starting transfers between devices  35.3 us (45%)
  waiting for transfers between devices  20.4 us (26%)
  Pallas kernels  16 us (21%)
  local copies, waits for them, and re-layouts  3.23 us (4%)
  other arithmetic  1.65 us (2%)
  between operations  0.8 us (1%)
    all_to_all x3, starting transfers between devices, exchange(): return lax.all_to_all(x, axes, 0, 0, tiled=True)  18.6 us
    all_to_all x3, waiting for transfers between devices, exchange(): return lax.all_to_all(x, axes, 0, 0, tiled=True)  16.2 us
    ppermute x6, starting transfers between devices, sent(): return lax.ppermute(block, AXES, route)  14.8 us
    pallas_call x1, Pallas kernels, layer(): pl.pallas_call(functools.partial(kernel, ua=ua, ub=ub, uc=uc, lock=lock),...  12.2 us
    ppermute x6, waiting for transfers between devices, sent(): return lax.ppermute(block, AXES, route)  4.17 us
    pallas_call x1, Pallas kernels, scatter(): pl.pallas_call(scatter_kernel, out_shape=(jax.ShapeDtypeStruct((256, 128)...  2.16 us
    ppermute x2, starting transfers between devices, passed_along(): lax.ppermute(block, SLAB, [(i, (i + distance) % count) for i in range(cou...  1.82 us
  transfers between devices with their start and end apart: 11, of which 5 were waited for; matrix products, arithmetic and copies ran while one was open for 3% of the time, Pallas kernels for 4%

profile of v3, /device:TPU:1, one launch (start us, length us, event | category | flops | bytes accessed | tf_op | source)
XLA Modules:
  0.0 77.4 jit_solution(6186452848111245722)
XLA Ops:
  0.6 0.0 copy-start.7
  0.7 0.1 pad.5.clone
  0.7 0.6 copy-done.7
  1.3 0.9 %maximum_maximum_fusion.b2 = bf16[144,128]{1,0:T(8,128)(2,1)S(1)} fusion(bf16[3,128]{1,0:T(4,128)(2,1)S(1)} %copy-done.7, bf16[128,128]{1,0:T(8,128)(2,1)} %param.11, bf16[144]{0:T(256)(128)(2,1)S(1)} %pad.5.clone), kind=kLoop, calls=%fused_computation.3 | loop fusion | flops 110592 | bytes 70688 | tf_op jit(solution)/shard_map/concatenate | solution.py:404
  2.2 4.4 %collective-permute-start.4 = (bf16[144,128]{1,0:T(8,128)(2,1)S(1)}, bf16[144,128]{1,0:T(8,128)(2,1)S(1)}, u32[]{:S(2)}, u32[]{:S(2)}) collective-permute-start(bf16[144,128]{1,0:T(8,128)(2,1)S(1)} %maximum_maximum_fusion.b2), channel_id=1, source_target_pairs={{0,255},{1,254},{2,1},{3,0},{4,3},{5,2},{6,5},{7,4},{8,7},{9,6},{1... | collective-permute-start | bytes 110600 | tf_op jit(solution)/shard_map/ppermute | solution.py:384
  6.6 7.1 %collective-permute-start.3 = (bf16[144,128]{1,0:T(8,128)(2,1)S(1)}, bf16[144,128]{1,0:T(8,128)(2,1)S(1)}, u32[]{:S(2)}, u32[]{:S(2)}) collective-permute-start(bf16[144,128]{1,0:T(8,128)(2,1)S(1)} %maximum_maximum_fusion.b2), channel_id=1, source_target_pairs={{0,254},{1,255},{2,0},{3,1},{4,2},{5,3},{6,4},{7,5},{8,6},{9,7},{1... | collective-permute-start | bytes 110600 | tf_op jit(solution)/shard_map/ppermute | solution.py:384
  13.7 0.4 collective-permute-start.2
  14.1 0.0 copy-start.6
  14.1 0.0 copy-start.1
  14.1 0.1 pad_add_fusion.place_ref
  14.2 0.6 copy-done.5
  14.8 0.1 copy-done.1
  14.8 0.0 copy-done.2
  14.8 1.0 %tables.1 = (f32[5,16,256]{2,1,0:T(8,128)S(1)}, f32[128,128]{1,0:T(8,128)S(1)}) custom-call(s32[3]{0:T(128)S(1)} %pad_add_fusion.place_ref, s32[32,128]{1,0:T(8,128)S(1)} %copy-done.1, s32[32,128]{1,0:T(8,128)S(1)} %copy-done.2, bf16[3,128]{1,0:T(4,128)(2,1)S(1)} %copy-done.5, f32[1,128]{1,0:T(1,128)S(1)} %bitcast.14), custom_call_target="tpu_custom_call" | custom-call | tf_op jit(solution)/shard_map/tables/pallas_call | solution.py:105
  15.9 2.4 %collective-permute-done.2.b3 = bf16[144,128]{1,0:T(8,128)(2,1)S(1)} collective-permute-done((bf16[144,128]{1,0:T(8,128)(2,1)S(1)}, bf16[144,128]{1,0:T(8,128)(2,1)S(1)}, u32[]{:S(2)}, u32[]{:S(2)}) %collective-permute-start.2) | collective-permute-done | bytes 36896 | tf_op jit(solution)/shard_map/ppermute | solution.py:384
  18.2 1.8 %collective-permute-done.1.b1 = bf16[144,128]{1,0:T(8,128)(2,1)S(1)} collective-permute-done((bf16[144,128]{1,0:T(8,128)(2,1)S(1)}, bf16[144,128]{1,0:T(8,128)(2,1)S(1)}, u32[]{:S(2)}, u32[]{:S(2)}) %collective-permute-start.1) | collective-permute-done | bytes 36896 | tf_op jit(solution)/shard_map/ppermute | solution.py:384
  20.0 12.2 %probe_layer.1 = (f32[8,128]{1,0:T(8,128)S(1)}, bf16[128,4096]{1,0:T(8,128)(2,1)S(1)}, f32[384,128]{1,0:T(8,128)}) custom-call(bf16[144,128]{1,0:T(8,128)(2,1)S(1)} %collective-permute-done.b0, bf16[144,128]{1,0:T(8,128)(2,1)S(1)} %collective-permute-done.1.b1, bf16[144,128]{1,0:T(8,128)(2,1)S(1)} %maximum_maximum_fusion.b2, ...), custom_call_target="tpu_custom_call" | custom-call | tf_op jit(solution)/shard_map/probe_layer/pallas_call | solution.py:311
  32.3 8.8 %all-to-all-start = ((f32[16,24,128]{2,1,0:T(8,128)}), f32[16,24,128]{2,1,0:T(8,128)S(1)}, u32[]{:S(2)}, u32[]{:S(2)}) async-start(f32[16,24,128]{2,1,0:T(8,128)} %bitcast.6), calls=%async_computation | async-start | bytes 393216 | tf_op jit(solution)/shard_map/all_to_all | solution.py:369
  41.0 2.2 %scatter_feat.1 = (bf16[256,128]{1,0:T(8,128)(2,1)S(1)}, bf16[256,128]{1,0:T(8,128)(2,1)S(1)}, bf16[256,128]{1,0:T(8,128)(2,1)S(1)}) custom-call(bf16[128,4096]{1,0:T(8,128)(2,1)S(1)} %get-tuple-element.19.gf_ref, f32[5,16,256]{2,1,0:T(8,128)S(1)} %get-tuple-element.16.tab_ref), custom_call_target="tpu_custom_call" | custom-call | tf_op jit(solution)/shard_map/scatter_feat/pallas_call | solution.py:298
  43.2 0.3 collective-permute-start.5
  43.5 1.5 %collective-permute-start.6 = (bf16[256,128]{1,0:T(8,128)(2,1)S(1)}, bf16[256,128]{1,0:T(8,128)(2,1)S(1)}, u32[]{:S(2)}, u32[]{:S(2)}) collective-permute-start(bf16[256,128]{1,0:T(8,128)(2,1)S(1)} %get-tuple-element.22), channel_id=1, source_target_pairs={{0,2},{2,4},{4,6},{6,8},{8,10},{10,12},{12,14},{14,16},{16,18},{18... | collective-permute-start | bytes 196616 | tf_op jit(solution)/shard_map/ppermute | solution.py:374
  45.0 2.7 %all-to-all-done = f32[16,24,128]{2,1,0:T(8,128)S(1)} async-done(((f32[16,24,128]{2,1,0:T(8,128)}), f32[16,24,128]{2,1,0:T(8,128)S(1)}, u32[]{:S(2)}, u32[]{:S(2)}) %all-to-all-start) | async-done | bytes 196640 | tf_op jit(solution)/shard_map/all_to_all | solution.py:369
  47.8 0.7 broadcast_in_dim.7
  48.4 3.8 %all-to-all-start.1 = ((f32[16,24,128]{2,1,0:T(8,128)}), f32[16,24,128]{2,1,0:T(8,128)S(1)}, u32[]{:S(2)}, u32[]{:S(2)}) async-start(f32[16,24,128]{2,1,0:T(8,128)} %broadcast_in_dim.7), calls=%async_computation.1 | async-start | bytes 393216 | tf_op jit(solution)/shard_map/all_to_all | solution.py:369
  52.3 3.0 %collective-permute-start.7 = (bf16[128,128]{1,0:T(8,128)(2,1)S(1)}, bf16[128,128]{1,0:T(8,128)(2,1)S(1)}, u32[]{:S(2)}, u32[]{:S(2)}) collective-permute-start(bf16[128,128]{1,0:T(8,128)(2,1)S(1)} %slice.18), channel_id=1, source_target_pairs={{0,1},{1,0},{2,3},{3,2},{4,5},{5,4},{6,7},{7,6},{8,9},{9,8},{10,11... | collective-permute-start | bytes 98312 | tf_op jit(solution)/shard_map/ppermute | solution.py:384
  55.3 0.5 slice_bitcast_fusion
  55.8 7.5 %all-to-all-done.1 = f32[16,24,128]{2,1,0:T(8,128)S(1)} async-done(((f32[16,24,128]{2,1,0:T(8,128)}), f32[16,24,128]{2,1,0:T(8,128)S(1)}, u32[]{:S(2)}, u32[]{:S(2)}) %all-to-all-start.1) | async-done | bytes 196640 | tf_op jit(solution)/shard_map/all_to_all | solution.py:369
  63.4 0.7 broadcast_in_dim.8
  64.0 6.0 %all-to-all-start.2 = ((f32[16,24,128]{2,1,0:T(8,128)}), f32[16,24,128]{2,1,0:T(8,128)S(1)}, u32[]{:S(2)}, u32[]{:S(2)}) async-start(f32[16,24,128]{2,1,0:T(8,128)} %broadcast_in_dim.8), calls=%async_computation.2 | async-start | bytes 393216 | tf_op jit(solution)/shard_map/all_to_all | solution.py:369
  70.1 0.6 slice_add_fusion
  70.7 6.0 %all-to-all-done.2 = f32[16,24,128]{2,1,0:T(8,128)S(1)} async-done(((f32[16,24,128]{2,1,0:T(8,128)}), f32[16,24,128]{2,1,0:T(8,128)S(1)}, u32[]{:S(2)}, u32[]{:S(2)}) %all-to-all-start.2) | async-done | bytes 196640 | tf_op jit(solution)/shard_map/all_to_all | solution.py:369
  76.7 0.7 finish.1
  (22 shorter events, 0.1 us)
Async XLA Ops:
  0.6 0.7 copy-start.7
  1.3 18.7 %copy-start = (bf16[640,64]{0,1:T(8,128)(2,1)S(1)}, bf16[640,64]{0,1:T(8,128)(2,1)}, u32[]{:S(2)}) copy-start(bf16[640,64]{0,1:T(8,128)(2,1)} %param.15) | copy-start | bytes 245764
  2.2 13.6 %collective-permute-start.4 = (bf16[144,128]{1,0:T(8,128)(2,1)S(1)}, bf16[144,128]{1,0:T(8,128)(2,1)S(1)}, u32[]{:S(2)}, u32[]{:S(2)}) collective-permute-start(bf16[144,128]{1,0:T(8,128)(2,1)S(1)} %maximum_maximum_fusion.b2), channel_id=1, source_target_pairs={{0,255},{1,254},{2,1},{3,0},{4,3},{5,2},{6,5},{7,4},{8,7},{9,6},{1... | collective-permute-start | bytes 110600 | tf_op jit(solution)/shard_map/ppermute | solution.py:384
  6.6 9.3 %collective-permute-start.3 = (bf16[144,128]{1,0:T(8,128)(2,1)S(1)}, bf16[144,128]{1,0:T(8,128)(2,1)S(1)}, u32[]{:S(2)}, u32[]{:S(2)}) collective-permute-start(bf16[144,128]{1,0:T(8,128)(2,1)S(1)} %maximum_maximum_fusion.b2), channel_id=1, source_target_pairs={{0,254},{1,255},{2,0},{3,1},{4,2},{5,3},{6,4},{7,5},{8,6},{9,7},{1... | collective-permute-start | bytes 110600 | tf_op jit(solution)/shard_map/ppermute | solution.py:384
  13.7 4.5 %collective-permute-start.2 = (bf16[144,128]{1,0:T(8,128)(2,1)S(1)}, bf16[144,128]{1,0:T(8,128)(2,1)S(1)}, u32[]{:S(2)}, u32[]{:S(2)}) collective-permute-start(bf16[144,128]{1,0:T(8,128)(2,1)S(1)} %maximum_maximum_fusion.b2), channel_id=1, source_target_pairs={{0,1},{1,0},{2,3},{3,2},{4,5},{5,4},{6,7},{7,6},{8,9},{9,8},{10,11... | collective-permute-start | bytes 110600 | tf_op jit(solution)/shard_map/ppermute | solution.py:384
  14.1 6.0 %collective-permute-start.1 = (bf16[144,128]{1,0:T(8,128)(2,1)S(1)}, bf16[144,128]{1,0:T(8,128)(2,1)S(1)}, u32[]{:S(2)}, u32[]{:S(2)}) collective-permute-start(bf16[144,128]{1,0:T(8,128)(2,1)S(1)} %maximum_maximum_fusion.b2), channel_id=1, source_target_pairs={{0,3},{1,2},{2,5},{3,4},{4,7},{5,6},{6,9},{7,8},{8,11},{9,10},{10,... | collective-permute-start | bytes 110600 | tf_op jit(solution)/shard_map/ppermute | solution.py:384
  14.1 6.0 %collective-permute-start = (bf16[144,128]{1,0:T(8,128)(2,1)S(1)}, bf16[144,128]{1,0:T(8,128)(2,1)S(1)}, u32[]{:S(2)}, u32[]{:S(2)}) collective-permute-start(bf16[144,128]{1,0:T(8,128)(2,1)S(1)} %maximum_maximum_fusion.b2), channel_id=1, source_target_pairs={{0,2},{1,3},{2,4},{3,5},{4,6},{5,7},{6,8},{7,9},{8,10},{9,11},{10,... | collective-permute-start | bytes 110600 | tf_op jit(solution)/shard_map/ppermute | solution.py:384
  14.1 0.7 copy-start.5
  14.1 0.7 copy-start.6
  14.1 0.7 copy-start.1
  14.1 0.7 copy-start.2
  14.8 5.2 %copy-start.4 = (f32[5,128]{1,0:T(8,128)S(1)}, f32[5,128]{1,0:T(8,128)}, u32[]{:S(2)}) copy-start(f32[5,128]{1,0:T(8,128)} %ro_ref.1) | copy-start | bytes 7684
  15.8 4.2 %copy-start.3 = (f32[64,8]{0,1:T(8,128)S(1)}, f32[64,8]{0,1:T(8,128)}, u32[]{:S(2)}) copy-start(f32[64,8]{0,1:T(8,128)} %param.14) | copy-start | bytes 6148
  32.3 15.5 %all-to-all-start = ((f32[16,24,128]{2,1,0:T(8,128)}), f32[16,24,128]{2,1,0:T(8,128)S(1)}, u32[]{:S(2)}, u32[]{:S(2)}) async-start(f32[16,24,128]{2,1,0:T(8,128)} %bitcast.6), calls=%async_computation | async-start | bytes 393216 | tf_op jit(solution)/shard_map/all_to_all | solution.py:369
  43.2 9.1 %collective-permute-start.5 = (bf16[256,128]{1,0:T(8,128)(2,1)S(1)}, bf16[256,128]{1,0:T(8,128)(2,1)S(1)}, u32[]{:S(2)}, u32[]{:S(2)}) collective-permute-start(bf16[256,128]{1,0:T(8,128)(2,1)S(1)} %get-tuple-element.21), channel_id=1, source_target_pairs={{0,254},{2,0},{4,2},{6,4},{8,6},{10,8},{12,10},{14,12},{16,14},{18... | collective-permute-start | bytes 196616 | tf_op jit(solution)/shard_map/ppermute | solution.py:374
  43.5 8.8 %collective-permute-start.6 = (bf16[256,128]{1,0:T(8,128)(2,1)S(1)}, bf16[256,128]{1,0:T(8,128)(2,1)S(1)}, u32[]{:S(2)}, u32[]{:S(2)}) collective-permute-start(bf16[256,128]{1,0:T(8,128)(2,1)S(1)} %get-tuple-element.22), channel_id=1, source_target_pairs={{0,2},{2,4},{4,6},{6,8},{8,10},{10,12},{12,14},{14,16},{16,18},{18... | collective-permute-start | bytes 196616 | tf_op jit(solution)/shard_map/ppermute | solution.py:374
  48.4 14.9 %all-to-all-start.1 = ((f32[16,24,128]{2,1,0:T(8,128)}), f32[16,24,128]{2,1,0:T(8,128)S(1)}, u32[]{:S(2)}, u32[]{:S(2)}) async-start(f32[16,24,128]{2,1,0:T(8,128)} %broadcast_in_dim.7), calls=%async_computation.1 | async-start | bytes 393216 | tf_op jit(solution)/shard_map/all_to_all | solution.py:369
  52.3 17.7 %collective-permute-start.7 = (bf16[128,128]{1,0:T(8,128)(2,1)S(1)}, bf16[128,128]{1,0:T(8,128)(2,1)S(1)}, u32[]{:S(2)}, u32[]{:S(2)}) collective-permute-start(bf16[128,128]{1,0:T(8,128)(2,1)S(1)} %slice.18), channel_id=1, source_target_pairs={{0,1},{1,0},{2,3},{3,2},{4,5},{5,4},{6,7},{7,6},{8,9},{9,8},{10,11... | collective-permute-start | bytes 98312 | tf_op jit(solution)/shard_map/ppermute | solution.py:384
  64.0 12.6 %all-to-all-start.2 = ((f32[16,24,128]{2,1,0:T(8,128)}), f32[16,24,128]{2,1,0:T(8,128)S(1)}, u32[]{:S(2)}, u32[]{:S(2)}) async-start(f32[16,24,128]{2,1,0:T(8,128)} %broadcast_in_dim.8), calls=%async_computation.2 | async-start | bytes 393216 | tf_op jit(solution)/shard_map/all_to_all | solution.py:369

commit v4 on v3

--- a/solution.py
+++ b/solution.py
@@ -305,7 +305,7 @@
     )(gf, tab)
 
 
-def layer(blocks, tab, w1t, w2t, ro, cot, ua=16, ub=16, uc=1, lock=4):
+def layer(blocks, tab, w1t, w2t, ro, cot, ua=16, ub=16, uc=2, lock=4):
     groups = tab.shape[1]
     edges = groups * 256
     return pl.pallas_call(

time: 77.9 us -> 77.6 us (level)
  no operation moved by 1% of the time
where the time goes in v4:
time: 77.6 us; the launch traced here: 77 us
  starting transfers between devices  35.3 us (45%)
  waiting for transfers between devices  20.4 us (26%)
  Pallas kernels  15.7 us (20%)
  local copies, waits for them, and re-layouts  3.23 us (4%)
  other arithmetic  1.65 us (2%)
  between operations  0.8 us (1%)
    all_to_all x3, starting transfers between devices, exchange(): return lax.all_to_all(x, axes, 0, 0, tiled=True)  18.6 us
    all_to_all x3, waiting for transfers between devices, exchange(): return lax.all_to_all(x, axes, 0, 0, tiled=True)  16.2 us
    ppermute x6, starting transfers between devices, sent(): return lax.ppermute(block, AXES, route)  14.8 us
    pallas_call x1, Pallas kernels, layer(): pl.pallas_call(functools.partial(kernel, ua=ua, ub=ub, uc=uc, lock=lock),...  11.9 us
    ppermute x6, waiting for transfers between devices, sent(): return lax.ppermute(block, AXES, route)  4.17 us
    pallas_call x1, Pallas kernels, scatter(): pl.pallas_call(scatter_kernel, out_shape=(jax.ShapeDtypeStruct((256, 128)...  2.16 us
    ppermute x2, starting transfers between devices, passed_along(): lax.ppermute(block, SLAB, [(i, (i + distance) % count) for i in range(cou...  1.82 us
  transfers between devices with their start and end apart: 11, of which 5 were waited for; matrix products, arithmetic and copies ran while one was open for 3% of the time, Pallas kernels for 4%

profile of v4, /device:TPU:1, one launch (start us, length us, event | category | flops | bytes accessed | tf_op | source)
XLA Modules:
  0.0 77.0 jit_solution(2032281406226678089)
XLA Ops:
  0.6 0.0 copy-start.7
  0.7 0.1 pad.5.clone
  0.7 0.6 copy-done.7
  1.3 0.9 %maximum_maximum_fusion.b2 = bf16[144,128]{1,0:T(8,128)(2,1)S(1)} fusion(bf16[3,128]{1,0:T(4,128)(2,1)S(1)} %copy-done.7, bf16[128,128]{1,0:T(8,128)(2,1)} %param.11, bf16[144]{0:T(256)(128)(2,1)S(1)} %pad.5.clone), kind=kLoop, calls=%fused_computation.3 | loop fusion | flops 110592 | bytes 70688 | tf_op jit(solution)/shard_map/concatenate | solution.py:404
  2.2 4.4 %collective-permute-start.4 = (bf16[144,128]{1,0:T(8,128)(2,1)S(1)}, bf16[144,128]{1,0:T(8,128)(2,1)S(1)}, u32[]{:S(2)}, u32[]{:S(2)}) collective-permute-start(bf16[144,128]{1,0:T(8,128)(2,1)S(1)} %maximum_maximum_fusion.b2), channel_id=1, source_target_pairs={{0,255},{1,254},{2,1},{3,0},{4,3},{5,2},{6,5},{7,4},{8,7},{9,6},{1... | collective-permute-start | bytes 110600 | tf_op jit(solution)/shard_map/ppermute | solution.py:384
  6.6 7.1 %collective-permute-start.3 = (bf16[144,128]{1,0:T(8,128)(2,1)S(1)}, bf16[144,128]{1,0:T(8,128)(2,1)S(1)}, u32[]{:S(2)}, u32[]{:S(2)}) collective-permute-start(bf16[144,128]{1,0:T(8,128)(2,1)S(1)} %maximum_maximum_fusion.b2), channel_id=1, source_target_pairs={{0,254},{1,255},{2,0},{3,1},{4,2},{5,3},{6,4},{7,5},{8,6},{9,7},{1... | collective-permute-start | bytes 110600 | tf_op jit(solution)/shard_map/ppermute | solution.py:384
  13.7 0.4 collective-permute-start.2
  14.1 0.0 copy-start.6
  14.1 0.0 copy-start.2
  14.1 0.1 pad_add_fusion.place_ref
  14.2 0.6 copy-done.5
  14.8 0.1 copy-done.1
  14.8 0.0 copy-done.2
  14.8 1.0 %tables.1 = (f32[5,16,256]{2,1,0:T(8,128)S(1)}, f32[128,128]{1,0:T(8,128)S(1)}) custom-call(s32[3]{0:T(128)S(1)} %pad_add_fusion.place_ref, s32[32,128]{1,0:T(8,128)S(1)} %copy-done.1, s32[32,128]{1,0:T(8,128)S(1)} %copy-done.2, bf16[3,128]{1,0:T(4,128)(2,1)S(1)} %copy-done.5, f32[1,128]{1,0:T(1,128)S(1)} %bitcast.14), custom_call_target="tpu_custom_call" | custom-call | tf_op jit(solution)/shard_map/tables/pallas_call | solution.py:105
  15.9 2.4 %collective-permute-done.2.b3 = bf16[144,128]{1,0:T(8,128)(2,1)S(1)} collective-permute-done((bf16[144,128]{1,0:T(8,128)(2,1)S(1)}, bf16[144,128]{1,0:T(8,128)(2,1)S(1)}, u32[]{:S(2)}, u32[]{:S(2)}) %collective-permute-start.2) | collective-permute-done | bytes 36896 | tf_op jit(solution)/shard_map/ppermute | solution.py:384
  18.2 1.8 %collective-permute-done.1.b1 = bf16[144,128]{1,0:T(8,128)(2,1)S(1)} collective-permute-done((bf16[144,128]{1,0:T(8,128)(2,1)S(1)}, bf16[144,128]{1,0:T(8,128)(2,1)S(1)}, u32[]{:S(2)}, u32[]{:S(2)}) %collective-permute-start.1) | collective-permute-done | bytes 36896 | tf_op jit(solution)/shard_map/ppermute | solution.py:384
  20.0 11.9 %probe_layer.1 = (f32[8,128]{1,0:T(8,128)S(1)}, bf16[128,4096]{1,0:T(8,128)(2,1)S(1)}, f32[384,128]{1,0:T(8,128)}) custom-call(bf16[144,128]{1,0:T(8,128)(2,1)S(1)} %collective-permute-done.b0, bf16[144,128]{1,0:T(8,128)(2,1)S(1)} %collective-permute-done.1.b1, bf16[144,128]{1,0:T(8,128)(2,1)S(1)} %maximum_maximum_fusion.b2, ...), custom_call_target="tpu_custom_call" | custom-call | tf_op jit(solution)/shard_map/probe_layer/pallas_call | solution.py:311
  31.9 8.8 %all-to-all-start = ((f32[16,24,128]{2,1,0:T(8,128)}), f32[16,24,128]{2,1,0:T(8,128)S(1)}, u32[]{:S(2)}, u32[]{:S(2)}) async-start(f32[16,24,128]{2,1,0:T(8,128)} %bitcast.6), calls=%async_computation | async-start | bytes 393216 | tf_op jit(solution)/shard_map/all_to_all | solution.py:369
  40.7 2.2 %scatter_feat.1 = (bf16[256,128]{1,0:T(8,128)(2,1)S(1)}, bf16[256,128]{1,0:T(8,128)(2,1)S(1)}, bf16[256,128]{1,0:T(8,128)(2,1)S(1)}) custom-call(bf16[128,4096]{1,0:T(8,128)(2,1)S(1)} %get-tuple-element.19.gf_ref, f32[5,16,256]{2,1,0:T(8,128)S(1)} %get-tuple-element.16.tab_ref), custom_call_target="tpu_custom_call" | custom-call | tf_op jit(solution)/shard_map/scatter_feat/pallas_call | solution.py:298
  42.9 0.5 collective-permute-start.5
  43.4 1.3 %collective-permute-start.6 = (bf16[256,128]{1,0:T(8,128)(2,1)S(1)}, bf16[256,128]{1,0:T(8,128)(2,1)S(1)}, u32[]{:S(2)}, u32[]{:S(2)}) collective-permute-start(bf16[256,128]{1,0:T(8,128)(2,1)S(1)} %get-tuple-element.22), channel_id=1, source_target_pairs={{0,2},{2,4},{4,6},{6,8},{8,10},{10,12},{12,14},{14,16},{16,18},{18... | collective-permute-start | bytes 196616 | tf_op jit(solution)/shard_map/ppermute | solution.py:374
  44.7 2.7 %all-to-all-done = f32[16,24,128]{2,1,0:T(8,128)S(1)} async-done(((f32[16,24,128]{2,1,0:T(8,128)}), f32[16,24,128]{2,1,0:T(8,128)S(1)}, u32[]{:S(2)}, u32[]{:S(2)}) %all-to-all-start) | async-done | bytes 196640 | tf_op jit(solution)/shard_map/all_to_all | solution.py:369
  47.4 0.7 broadcast_in_dim.7
  48.1 3.8 %all-to-all-start.1 = ((f32[16,24,128]{2,1,0:T(8,128)}), f32[16,24,128]{2,1,0:T(8,128)S(1)}, u32[]{:S(2)}, u32[]{:S(2)}) async-start(f32[16,24,128]{2,1,0:T(8,128)} %broadcast_in_dim.7), calls=%async_computation.1 | async-start | bytes 393216 | tf_op jit(solution)/shard_map/all_to_all | solution.py:369
  52.0 3.0 %collective-permute-start.7 = (bf16[128,128]{1,0:T(8,128)(2,1)S(1)}, bf16[128,128]{1,0:T(8,128)(2,1)S(1)}, u32[]{:S(2)}, u32[]{:S(2)}) collective-permute-start(bf16[128,128]{1,0:T(8,128)(2,1)S(1)} %slice.18), channel_id=1, source_target_pairs={{0,1},{1,0},{2,3},{3,2},{4,5},{5,4},{6,7},{7,6},{8,9},{9,8},{10,11... | collective-permute-start | bytes 98312 | tf_op jit(solution)/shard_map/ppermute | solution.py:384
  55.0 0.5 slice_bitcast_fusion
  55.5 7.5 %all-to-all-done.1 = f32[16,24,128]{2,1,0:T(8,128)S(1)} async-done(((f32[16,24,128]{2,1,0:T(8,128)}), f32[16,24,128]{2,1,0:T(8,128)S(1)}, u32[]{:S(2)}, u32[]{:S(2)}) %all-to-all-start.1) | async-done | bytes 196640 | tf_op jit(solution)/shard_map/all_to_all | solution.py:369
  63.0 0.7 broadcast_in_dim.8
  63.7 6.0 %all-to-all-start.2 = ((f32[16,24,128]{2,1,0:T(8,128)}), f32[16,24,128]{2,1,0:T(8,128)S(1)}, u32[]{:S(2)}, u32[]{:S(2)}) async-start(f32[16,24,128]{2,1,0:T(8,128)} %broadcast_in_dim.8), calls=%async_computation.2 | async-start | bytes 393216 | tf_op jit(solution)/shard_map/all_to_all | solution.py:369
  69.7 0.6 slice_add_fusion
  70.4 6.0 %all-to-all-done.2 = f32[16,24,128]{2,1,0:T(8,128)S(1)} async-done(((f32[16,24,128]{2,1,0:T(8,128)}), f32[16,24,128]{2,1,0:T(8,128)S(1)}, u32[]{:S(2)}, u32[]{:S(2)}) %all-to-all-start.2) | async-done | bytes 196640 | tf_op jit(solution)/shard_map/all_to_all | solution.py:369
  76.4 0.7 finish.1
  (22 shorter events, 0.1 us)
Async XLA Ops:
  0.6 0.7 copy-start.7
  1.3 18.7 %copy-start = (bf16[640,64]{0,1:T(8,128)(2,1)S(1)}, bf16[640,64]{0,1:T(8,128)(2,1)}, u32[]{:S(2)}) copy-start(bf16[640,64]{0,1:T(8,128)(2,1)} %param.15) | copy-start | bytes 245764
  2.2 13.6 %collective-permute-start.4 = (bf16[144,128]{1,0:T(8,128)(2,1)S(1)}, bf16[144,128]{1,0:T(8,128)(2,1)S(1)}, u32[]{:S(2)}, u32[]{:S(2)}) collective-permute-start(bf16[144,128]{1,0:T(8,128)(2,1)S(1)} %maximum_maximum_fusion.b2), channel_id=1, source_target_pairs={{0,255},{1,254},{2,1},{3,0},{4,3},{5,2},{6,5},{7,4},{8,7},{9,6},{1... | collective-permute-start | bytes 110600 | tf_op jit(solution)/shard_map/ppermute | solution.py:384
  6.6 9.3 %collective-permute-start.3 = (bf16[144,128]{1,0:T(8,128)(2,1)S(1)}, bf16[144,128]{1,0:T(8,128)(2,1)S(1)}, u32[]{:S(2)}, u32[]{:S(2)}) collective-permute-start(bf16[144,128]{1,0:T(8,128)(2,1)S(1)} %maximum_maximum_fusion.b2), channel_id=1, source_target_pairs={{0,254},{1,255},{2,0},{3,1},{4,2},{5,3},{6,4},{7,5},{8,6},{9,7},{1... | collective-permute-start | bytes 110600 | tf_op jit(solution)/shard_map/ppermute | solution.py:384
  13.7 4.5 %collective-permute-start.2 = (bf16[144,128]{1,0:T(8,128)(2,1)S(1)}, bf16[144,128]{1,0:T(8,128)(2,1)S(1)}, u32[]{:S(2)}, u32[]{:S(2)}) collective-permute-start(bf16[144,128]{1,0:T(8,128)(2,1)S(1)} %maximum_maximum_fusion.b2), channel_id=1, source_target_pairs={{0,1},{1,0},{2,3},{3,2},{4,5},{5,4},{6,7},{7,6},{8,9},{9,8},{10,11... | collective-permute-start | bytes 110600 | tf_op jit(solution)/shard_map/ppermute | solution.py:384
  14.1 6.0 %collective-permute-start.1 = (bf16[144,128]{1,0:T(8,128)(2,1)S(1)}, bf16[144,128]{1,0:T(8,128)(2,1)S(1)}, u32[]{:S(2)}, u32[]{:S(2)}) collective-permute-start(bf16[144,128]{1,0:T(8,128)(2,1)S(1)} %maximum_maximum_fusion.b2), channel_id=1, source_target_pairs={{0,3},{1,2},{2,5},{3,4},{4,7},{5,6},{6,9},{7,8},{8,11},{9,10},{10,... | collective-permute-start | bytes 110600 | tf_op jit(solution)/shard_map/ppermute | solution.py:384
  14.1 6.0 %collective-permute-start = (bf16[144,128]{1,0:T(8,128)(2,1)S(1)}, bf16[144,128]{1,0:T(8,128)(2,1)S(1)}, u32[]{:S(2)}, u32[]{:S(2)}) collective-permute-start(bf16[144,128]{1,0:T(8,128)(2,1)S(1)} %maximum_maximum_fusion.b2), channel_id=1, source_target_pairs={{0,2},{1,3},{2,4},{3,5},{4,6},{5,7},{6,8},{7,9},{8,10},{9,11},{10,... | collective-permute-start | bytes 110600 | tf_op jit(solution)/shard_map/ppermute | solution.py:384
  14.1 0.7 copy-start.5
  14.1 0.7 copy-start.6
  14.1 0.7 copy-start.1
  14.1 0.7 copy-start.2
  14.8 5.2 %copy-start.4 = (f32[5,128]{1,0:T(8,128)S(1)}, f32[5,128]{1,0:T(8,128)}, u32[]{:S(2)}) copy-start(f32[5,128]{1,0:T(8,128)} %ro_ref.1) | copy-start | bytes 7684
  15.8 4.2 %copy-start.3 = (f32[64,8]{0,1:T(8,128)S(1)}, f32[64,8]{0,1:T(8,128)}, u32[]{:S(2)}) copy-start(f32[64,8]{0,1:T(8,128)} %param.14) | copy-start | bytes 6148
  31.9 15.5 %all-to-all-start = ((f32[16,24,128]{2,1,0:T(8,128)}), f32[16,24,128]{2,1,0:T(8,128)S(1)}, u32[]{:S(2)}, u32[]{:S(2)}) async-start(f32[16,24,128]{2,1,0:T(8,128)} %bitcast.6), calls=%async_computation | async-start | bytes 393216 | tf_op jit(solution)/shard_map/all_to_all | solution.py:369
  42.9 9.1 %collective-permute-start.5 = (bf16[256,128]{1,0:T(8,128)(2,1)S(1)}, bf16[256,128]{1,0:T(8,128)(2,1)S(1)}, u32[]{:S(2)}, u32[]{:S(2)}) collective-permute-start(bf16[256,128]{1,0:T(8,128)(2,1)S(1)} %get-tuple-element.21), channel_id=1, source_target_pairs={{0,254},{2,0},{4,2},{6,4},{8,6},{10,8},{12,10},{14,12},{16,14},{18... | collective-permute-start | bytes 196616 | tf_op jit(solution)/shard_map/ppermute | solution.py:374
  43.4 8.6 %collective-permute-start.6 = (bf16[256,128]{1,0:T(8,128)(2,1)S(1)}, bf16[256,128]{1,0:T(8,128)(2,1)S(1)}, u32[]{:S(2)}, u32[]{:S(2)}) collective-permute-start(bf16[256,128]{1,0:T(8,128)(2,1)S(1)} %get-tuple-element.22), channel_id=1, source_target_pairs={{0,2},{2,4},{4,6},{6,8},{8,10},{10,12},{12,14},{14,16},{16,18},{18... | collective-permute-start | bytes 196616 | tf_op jit(solution)/shard_map/ppermute | solution.py:374
  48.1 14.9 %all-to-all-start.1 = ((f32[16,24,128]{2,1,0:T(8,128)}), f32[16,24,128]{2,1,0:T(8,128)S(1)}, u32[]{:S(2)}, u32[]{:S(2)}) async-start(f32[16,24,128]{2,1,0:T(8,128)} %broadcast_in_dim.7), calls=%async_computation.1 | async-start | bytes 393216 | tf_op jit(solution)/shard_map/all_to_all | solution.py:369
  52.0 17.7 %collective-permute-start.7 = (bf16[128,128]{1,0:T(8,128)(2,1)S(1)}, bf16[128,128]{1,0:T(8,128)(2,1)S(1)}, u32[]{:S(2)}, u32[]{:S(2)}) collective-permute-start(bf16[128,128]{1,0:T(8,128)(2,1)S(1)} %slice.18), channel_id=1, source_target_pairs={{0,1},{1,0},{2,3},{3,2},{4,5},{5,4},{6,7},{7,6},{8,9},{9,8},{10,11... | collective-permute-start | bytes 98312 | tf_op jit(solution)/shard_map/ppermute | solution.py:384
  63.7 12.6 %all-to-all-start.2 = ((f32[16,24,128]{2,1,0:T(8,128)}), f32[16,24,128]{2,1,0:T(8,128)S(1)}, u32[]{:S(2)}, u32[]{:S(2)}) async-start(f32[16,24,128]{2,1,0:T(8,128)} %broadcast_in_dim.8), calls=%async_computation.2 | async-start | bytes 393216 | tf_op jit(solution)/shard_map/all_to_all | solution.py:369
